TPU v7x, 512 devices: a whole 4x8x8 slice. The times are simulated.
512 devices in a mesh: area: 64 (over y, x, core), snap: 8 (over z).
Axes of the slice: x: 4, y: 8, z: 8, core: 2. Of those that a mesh axis runs over, the one named last changes fastest.
Arguments:
- phasor_readings: float32 [256, 131072], P('snap', 'area')
- reading_error_spread: float32 [131072], P('area'), may hold values from 1 to 100
- starting_voltages: float32 [256, 131072], P('snap', 'area'), may hold values from -6 to 6
- derivative_pieces: bfloat16 [1024, 4, 128, 128], P('area'), may hold values from -0.25 to 0.25
- derivative_tile_position: int32 [64, 16, 4], P('area'), may hold values from 0 to 23, as said below
- frontier_voltage_pieces: int32 [64, 2, 4], P('area'), may hold values from -1 to 15, as said below
- holder_line_order: int32 [64, 64, 64], P('area'), may hold values from -1 to 2047, as said below
- hub_line_order: int32 [64, 64, 64], P('area'), may hold values from -1 to 2047, as said below
- reciprocal_normal_operator: bfloat16 [131072, 2048], P(('area', 'snap'))
Outputs:
- state: float32 [256, 131072], P('snap', 'area')
Inputs may be any that keep to these rules, and one draw needn't show every extreme that they name: holder_line_order[d, c] lists the owner rows of area d that concentrator c handles, at most 64 of them, then -1; every owner row appears exactly once over all concentrators; some pair holds exactly 64. hub_line_order[c, d] lists the rows of concentrator c matching holder_line_order[d, c] entry by entry, with -1 at the same places; every concentrator row appears exactly once. `derivative_tile_position`: the 4 slots of one measurement block are distinct. frontier_voltage_pieces[a, 0] lists distinct blocks sent to area a - 1 and frontier_voltage_pieces[a, 1] those sent to area a + 1, 1 to 4 of them then -1; the list of area 0 toward lower and of the last area toward upper are all -1; some list holds 4.
All inputs are finite; a program needn't handle non-finite values.
Results may differ from a plain program's by a relative error of at most 0.0022.
Values may be sent and summed in bfloat16 or wider, within the bound.
A program may use at most 64 MiB of HBM per device.

v0:
```python
import jax
import jax.numpy as jnp
from jax import lax
from jax.sharding import PartitionSpec as P

NS = 2048
BLK = 128
MEASURE_BLOCKS = 16
TOUCHED_BLOCKS = 4
TIES = 4
ITERS = 2
NB = 16
SLOT_COUNT = 24
READING_LINES = 2048


HIGHEST_PRECISION = lax.Precision.HIGHEST


def passed_along(block, axis, distance):
    devices = range(lax.axis_size(axis))
    route = [(i - distance, i) for i in devices if i - distance in devices]
    return lax.ppermute(block, axis, route)


def block_lookup(listing, total_blocks):
    return (listing[:, None] == jnp.arange(total_blocks, dtype=jnp.int32)[None, :]).astype(
        jnp.float32
    )


def pick_blocks(blocks, listing):
    onehot_table = block_lookup(listing, blocks.shape[1])
    return jnp.einsum("tb,sbc->stc", onehot_table, blocks, precision=HIGHEST_PRECISION)


def place_blocks(values, listing, total_blocks):
    onehot_table = block_lookup(listing, total_blocks)
    return jnp.einsum("stc,tb->sbc", values, onehot_table, precision=HIGHEST_PRECISION)


def pass_states(values, offset):
    return passed_along(values.astype(jnp.bfloat16), "area", offset).astype(values.dtype)


def return_grads(values, offset):
    return passed_along(values, "area", offset)


def snapshot_total(partial_sum):
    return lax.psum(partial_sum, "snap")


def on_device(
    phasor_readings,
    reading_error_spread,
    starting_voltages,
    derivative_pieces,
    derivative_tile_position,
    frontier_voltage_pieces,
    holder_line_order,
    hub_line_order,
    reciprocal_normal_operator,
):
    snap_dev = starting_voltages.shape[0]
    snaps_all = snap_dev * lax.axis_size("snap")
    slot_column_index = derivative_tile_position[0]
    ties_lower = frontier_voltage_pieces[0, 0]
    ties_upper = frontier_voltage_pieces[0, 1]
    own_flat = holder_line_order[0].reshape(-1)
    own_valid = own_flat >= 0
    own_gather = jnp.where(own_valid, own_flat, 0)
    own_place = jnp.where(own_valid, own_flat, READING_LINES)
    conc_flat = hub_line_order[0].reshape(-1)
    conc_valid = conc_flat >= 0
    hub_pickup = jnp.where(conc_valid, conc_flat, 0)
    slot_lookup = block_lookup(slot_column_index.reshape(-1), SLOT_COUNT)
    hub_readings = jnp.take(phasor_readings, hub_pickup, axis=1)
    collector_variance = jnp.take(reading_error_spread, hub_pickup)
    current = starting_voltages
    for step_index in range(ITERS):
        blocks = current.reshape(snap_dev, NB, BLK)
        from_below = pass_states(pick_blocks(blocks, ties_upper), 1)
        from_above = pass_states(pick_blocks(blocks, ties_lower), -1)
        augmented = jnp.concatenate([blocks, from_below, from_above], axis=1).astype(jnp.bfloat16)
        chosen = jnp.take(augmented, slot_column_index, axis=1)
        predicted = jnp.einsum(
            "jkrc,sjkc->sjr", derivative_pieces, chosen, preferred_element_type=jnp.float32
        ).reshape(snap_dev, READING_LINES)
        outgoing = jnp.where(own_valid[None, :], jnp.take(predicted, own_gather, axis=1), 0.0)
        incoming_blocks = lax.all_to_all(outgoing, "area", split_axis=1, concat_axis=1, tiled=True)
        residual_rows = hub_readings - incoming_blocks
        spread = snapshot_total(jnp.sum(residual_rows * residual_rows, axis=0)) / snaps_all
        scaled = jnp.where(
            conc_valid[None, :],
            residual_rows / (collector_variance[None, :] + spread[None, :]),
            0.0,
        ).astype(jnp.bfloat16)
        returned = lax.all_to_all(scaled, "area", split_axis=1, concat_axis=1, tiled=True)
        weighted = (
            jnp.zeros((snap_dev, READING_LINES), jnp.bfloat16)
            .at[:, own_place]
            .set(returned, mode="drop")
        )
        tile_grad = jnp.einsum(
            "jkrc,sjr->sjkc",
            derivative_pieces,
            weighted.reshape(snap_dev, MEASURE_BLOCKS, BLK),
            preferred_element_type=jnp.float32,
        )
        slot_grad = jnp.einsum(
            "sxc,xn->snc",
            tile_grad.reshape(snap_dev, MEASURE_BLOCKS * TOUCHED_BLOCKS, BLK),
            slot_lookup,
            precision=HIGHEST_PRECISION,
        )
        back_upper = return_grads(slot_grad[:, NB : NB + TIES], -1)
        back_lower = return_grads(slot_grad[:, NB + TIES :], 1)
        gradient = (
            slot_grad[:, :NB]
            + place_blocks(back_upper, ties_upper, NB)
            + place_blocks(back_lower, ties_lower, NB)
        )
        flat_grad = gradient.reshape(snap_dev, NS).astype(jnp.bfloat16)
        rows_all = jnp.einsum(
            "se,ie->si",
            lax.all_gather(flat_grad, "snap", axis=0, tiled=True),
            reciprocal_normal_operator,
            preferred_element_type=jnp.float32,
        )
        update = lax.all_to_all(rows_all, "snap", split_axis=0, concat_axis=1, tiled=True)
        current = current + update
    return current


def solution(mesh):
    placed = (
        P("snap", "area"),
        P("area"),
        P("snap", "area"),
        P("area", None, None, None),
        P("area", None, None),
        P("area", None, None),
        P("area", None, None),
        P("area", None, None),
        P(("area", "snap"), None),
    )
    return jax.shard_map(
        on_device, mesh=mesh, in_specs=placed, out_specs=P("snap", "area"), check_vma=False
    )
```

profile of v0, /device:TPU:4, one launch (start us, length us, event | category | flops | bytes accessed | tf_op | source)
XLA Modules:
  0.0 467.8 jit_solution(10735887621970210297)
XLA Ops:
  8.7 1.9 collective-permute-start.1
  10.8 2.4 collective-permute-start
  19.6 14.1 %gather_fusion.3 = f32[4096,32]{1,0:T(8,128)} fusion(f32[32,2048]{0,1:T(8,128)S(1)} %bitcast.186, s32[4096]{0:T(1024)S(1)} %fusion.28), kind=kCustom, calls=%fused_computation.2.clone | custom fusion | bytes 1064960 | tf_op jit(solution)/shard_map/jit(_take)/gather | solution.py:90
  33.7 6.0 %bitcast_select_fusion.1 = f32[32,4096]{0,1:T(8,128)} fusion(f32[4096,32]{1,0:T(8,128)} %gather_fusion.3, pred[4096]{0:T(1024)(128)(4,1)S(1)} %get-tuple-element.14, pred[4096]{0:T(1024)(128)(4,1)S(1)} %get-tuple-element.13), kind=kLoop, calls=%fused_computation.11 | loop fusion | flops 262144 | bytes 1056768 | tf_op jit(solution)/shard_map/jit(_where)/select_n | solution.py:90
  39.7 2.2 copy.107
  41.9 1.5 reshape.235
  43.4 13.3 %all-to-all-start = ((f32[64,1,2048]{2,1,0:T(1,128)}), f32[64,1,2048]{2,1,0:T(1,128)}, u32[]{:S(2)}, u32[]{:S(2)}) async-start(f32[64,1,2048]{2,1,0:T(1,128)} %reshape.235), calls=%async_computation | async-start | bytes 1048576 | tf_op jit(solution)/shard_map/all_to_all | solution.py:91
  57.5 23.0 %gather_fusion = f32[4096]{0:T(1024)S(1)} fusion(f32[2048]{0:T(1024)S(1)} %copy-done.1, s32[4096]{0:T(1024)S(1)} %broadcast_clamp_fusion), kind=kCustom, calls=%fused_computation.5 | custom fusion | bytes 49152 | tf_op jit(solution)/shard_map/jit(_take)/gather | solution.py:79
  80.5 14.1 %gather_fusion.1 = f32[4096,32]{1,0:T(8,128)} fusion(f32[32,2048]{0,1:T(8,128)S(1)} %copy.99, s32[4096]{0:T(1024)S(1)} %fusion.27), kind=kCustom, calls=%fused_computation.clone | custom fusion | bytes 1064960 | tf_op jit(solution)/shard_map/jit(_take)/gather | solution.py:78
  95.2 3.7 reduce
  99.0 1.5 reshape.236
  100.4 2.0 copy.108
  102.4 2.8 multiply_reduce_fusion.1
  105.2 35.9 %psum.14 = f32[4096]{0:T(1024)S(1)} all-reduce(f32[4096]{0:T(1024)S(1)} %multiply_reduce_fusion.1), channel_id=1, replica_groups=mesh['area'=64,'snap'=8] {'snap'}, use_global_device_ids=true, to_apply=%region_1.4 | all-reduce | flops 4096 | bytes 32768 | tf_op jit(solution)/shard_map/psum | solution.py:51
  141.2 6.4 %select_convert_fusion.1 = bf16[32,4096]{0,1:T(8,128)(2,1)S(1)} fusion(f32[4096]{0:T(1024)S(1)} %multiply_add_fusion.1, pred[4096]{0:T(1024)(128)(4,1)S(1)} %get-tuple-element.11, f32[32,64,64]{0,2,1:T(8,128)} %copy.108, f32[4096,32]{1,0:T(8,128)} %gather_fusion.1, pred[4096]{0:T(1024)(128)(4,1)S(1)} %get-tuple-element.12), kind=kLoop, calls=%fused_computation.14 | loop fusion | flops 655360 | bytes 1335296 | tf_op jit(solution)/shard_map/convert_element_type | solution.py:98
  148.7 2.1 reshape.237
  150.8 10.3 %all-to-all-start.1 = ((bf16[64,2,1024]{2,1,0:T(2,128)(2,1)}), bf16[64,2,1024]{2,1,0:T(2,128)(2,1)S(1)}, u32[]{:S(2)}, u32[]{:S(2)}) async-start(bf16[64,2,1024]{2,1,0:T(2,128)(2,1)} %reshape.237), calls=%async_computation.1 | async-start | bytes 524288 | tf_op jit(solution)/shard_map/all_to_all | solution.py:99
  161.4 11.7 %all-to-all-done.1 = bf16[64,2,1024]{2,1,0:T(2,128)(2,1)S(1)} async-done(((bf16[64,2,1024]{2,1,0:T(2,128)(2,1)}), bf16[64,2,1024]{2,1,0:T(2,128)(2,1)S(1)}, u32[]{:S(2)}, u32[]{:S(2)}) %all-to-all-start.1) | async-done | bytes 262176 | tf_op jit(solution)/shard_map/all_to_all | solution.py:99
  175.3 11.2 %scatter_custom_fusion = bf16[32,2048]{0,1:T(8,128)(2,1)S(1)} fusion(s32[4096]{0:T(1024)S(1)} %bitcast.224, bf16[4096,32]{1,0:T(8,128)(2,1)} %copy.111, bf16[]{:T(256)} %constant.23.clone.1), kind=kCustom, calls=%fused_computation.52 | custom fusion | bytes 131584 | tf_op jit(solution)/shard_map/scatter | solution.py:103
  188.2 2.5 collective-permute-start.2
  190.7 1.9 collective-permute-start.3
  193.1 3.2 collective-permute-done.3
  197.5 38.6 %all-gather.3.cloned.1.call-done = bf16[256,2048]{1,0:T(8,128)(2,1)} async-done(((bf16[32,2048]{1,0:T(8,128)(2,1)}), bf16[256,2048]{1,0:T(8,128)(2,1)}) %all-gather.3.cloned.1.call-update) | async-done | bytes 1048592 | tf_op jit(solution)/shard_map/all_gather | solution.py:127
  236.1 1.7 fusion.46
  237.8 14.4 %all_to_all.86 = f32[8,32,256]{2,1,0:T(8,128)S(1)} all-to-all(f32[8,32,256]{2,1,0:T(8,128)S(1)} %bitcast.214), channel_id=1, replica_groups=mesh['area'=64,'snap'=8] {'snap'}, dimensions={0} | all-to-all | bytes 524288 | tf_op jit(solution)/shard_map/all_to_all | solution.py:131
  253.7 1.9 collective-permute-start.5
  255.7 2.4 collective-permute-start.4
  258.1 2.8 collective-permute-done.4
  261.6 1.5 convolution_bitcast_fusion.4
  264.5 14.1 %gather_fusion.5 = f32[4096,32]{1,0:T(8,128)} fusion(f32[32,2048]{0,1:T(8,128)S(1)} %bitcast.185, s32[4096]{0:T(1024)S(1)} %fusion.28), kind=kCustom, calls=%fused_computation.3.clone | custom fusion | bytes 1064960 | tf_op jit(solution)/shard_map/jit(_take)/gather | solution.py:90
  278.6 6.0 %bitcast_select_fusion = f32[32,4096]{0,1:T(8,128)} fusion(f32[4096,32]{1,0:T(8,128)} %gather_fusion.5, pred[4096]{0:T(1024)(128)(4,1)S(1)} %copy-done.8, pred[4096]{0:T(1024)(128)(4,1)S(1)} %get-tuple-element.13), kind=kLoop, calls=%fused_computation.9 | loop fusion | flops 262144 | bytes 1056768 | tf_op jit(solution)/shard_map/jit(_where)/select_n | solution.py:90
  284.5 2.2 copy.122
  286.7 1.5 reshape.239
  288.2 28.7 %all_to_all.87 = f32[64,1,2048]{2,1,0:T(1,128)S(1)} all-to-all(f32[64,1,2048]{2,1,0:T(1,128)} %reshape.239), channel_id=1, replica_groups=mesh['area'=64,'snap'=8] {'area'}, dimensions={0} | all-to-all | bytes 1048576 | tf_op jit(solution)/shard_map/all_to_all | solution.py:91
  316.9 2.8 reduce.1
  319.7 1.5 reshape.240
  321.1 2.0 copy.123
  323.1 2.8 multiply_reduce_fusion
  325.9 27.1 %psum.15 = f32[4096]{0:T(1024)S(1)} all-reduce(f32[4096]{0:T(1024)S(1)} %multiply_reduce_fusion), channel_id=1, replica_groups=mesh['area'=64,'snap'=8] {'snap'}, use_global_device_ids=true, to_apply=%region_4.7 | all-reduce | flops 4096 | bytes 32768 | tf_op jit(solution)/shard_map/psum | solution.py:51
  353.0 6.4 %select_convert_fusion = bf16[32,4096]{0,1:T(8,128)(2,1)S(1)} fusion(f32[4096]{0:T(1024)S(1)} %multiply_add_fusion, pred[4096]{0:T(1024)(128)(4,1)S(1)} %get-tuple-element.11, f32[32,64,64]{0,2,1:T(8,128)} %copy.123, f32[4096,32]{1,0:T(8,128)} %gather_fusion.1, pred[4096]{0:T(1024)(128)(4,1)S(1)} %get-tuple-element.12), kind=kLoop, calls=%fused_computation.12 | loop fusion | flops 655360 | bytes 1335296 | tf_op jit(solution)/shard_map/convert_element_type | solution.py:98
  361.9 17.6 %all_to_all.88 = bf16[64,2,1024]{2,1,0:T(2,128)(2,1)S(1)} all-to-all(bf16[64,2,1024]{2,1,0:T(2,128)(2,1)S(1)} %reshape.241), channel_id=1, replica_groups=mesh['area'=64,'snap'=8] {'area'}, dimensions={0} | all-to-all | bytes 524288 | tf_op jit(solution)/shard_map/all_to_all | solution.py:99
  381.8 11.2 %scatter_custom_fusion.1 = bf16[32,2048]{0,1:T(8,128)(2,1)S(1)} fusion(s32[4096]{0:T(1024)S(1)} %bitcast.225, bf16[4096,32]{1,0:T(8,128)(2,1)} %copy.126, bf16[]{:T(256)} %constant.23.clone.1), kind=kCustom, calls=%fused_computation.50 | custom fusion | bytes 131584 | tf_op jit(solution)/shard_map/scatter | solution.py:103
  394.6 2.5 collective-permute-start.6
  397.1 1.9 collective-permute-start.7
  399.5 3.2 collective-permute-done.7
  403.9 40.3 %all-gather.5.cloned.1.call-done = bf16[256,2048]{1,0:T(8,128)(2,1)} async-done(((bf16[32,2048]{1,0:T(8,128)(2,1)}), bf16[256,2048]{1,0:T(8,128)(2,1)}) %all-gather.5.cloned.1.call-update) | async-done | bytes 1048592 | tf_op jit(solution)/shard_map/all_gather | solution.py:127
  444.1 1.7 fusion.48
  445.8 14.4 %all_to_all.89 = f32[8,32,256]{2,1,0:T(8,128)S(1)} all-to-all(f32[8,32,256]{2,1,0:T(8,128)S(1)} %bitcast.216), channel_id=1, replica_groups=mesh['area'=64,'snap'=8] {'snap'}, dimensions={0} | all-to-all | bytes 524288 | tf_op jit(solution)/shard_map/all_to_all | solution.py:131
  (112 shorter events, 29.0 us)
Async XLA Ops:
  6.5 11.8 %copy-start = (bf16[16,4,128,128]{3,2,1,0:T(8,128)(2,1)S(1)}, bf16[16,4,128,128]{3,2,1,0:T(8,128)(2,1)}, u32[]{:S(2)}) copy-start(bf16[16,4,128,128]{3,2,1,0:T(8,128)(2,1)} %param.16) | copy-start | bytes 6291460
  7.4 6.6 %copy-start.12 = (s32[4]{0:T(128)}, s32[4]{0:T(128)S(1)}, u32[]{:S(2)}) copy-start(s32[4]{0:T(128)S(1)} %get-tuple-element.16) | copy-start | bytes 52
  7.4 9.2 %copy-start.14 = (s32[4]{0:T(128)}, s32[4]{0:T(128)S(1)}, u32[]{:S(2)}) copy-start(s32[4]{0:T(128)S(1)} %get-tuple-element.15) | copy-start | bytes 52
  8.7 9.0 %collective-permute-start.1 = (bf16[32,4,128]{2,1,0:T(4,128)(2,1)S(1)}, bf16[32,4,128]{2,1,0:T(4,128)(2,1)S(1)}, u32[]{:S(2)}, u32[]{:S(2)}) collective-permute-start(bf16[32,4,128]{2,1,0:T(4,128)(2,1)S(1)} %fusion.7), channel_id=1, source_target_pairs={{8,0},{16,8},{24,16},{32,24},{40,32},{48,40},{56,48},{64,56},{72,6... | collective-permute-start | bytes 98312 | tf_op jit(solution)/shard_map/ppermute | solution.py:23
  10.8 6.8 %collective-permute-start = (bf16[32,4,128]{2,1,0:T(4,128)(2,1)S(1)}, bf16[32,4,128]{2,1,0:T(4,128)(2,1)S(1)}, u32[]{:S(2)}, u32[]{:S(2)}) collective-permute-start(bf16[32,4,128]{2,1,0:T(4,128)(2,1)S(1)} %fusion.6), channel_id=1, source_target_pairs={{0,8},{8,16},{16,24},{24,32},{32,40},{40,48},{48,56},{56,64},{64,7... | collective-permute-start | bytes 98312 | tf_op jit(solution)/shard_map/ppermute | solution.py:23
  15.5 18.2 %copy-start.7 = (pred[4096]{0:T(1024)(128)(4,1)}, pred[4096]{0:T(1024)(128)(4,1)S(1)}, u32[]{:S(2)}) copy-start(pred[4096]{0:T(1024)(128)(4,1)S(1)} %get-tuple-element.14) | copy-start | bytes 12292
  16.8 2.4 copy-start.9
  41.9 14.9 %copy-start.11 = (s32[1,16,4]{1,2,0:T(4,128)S(1)}, s32[1,16,4]{1,2,0:T(4,128)}, u32[]{:S(2)}) copy-start(s32[1,16,4]{1,2,0:T(4,128)} %param.17) | copy-start | bytes 772
  41.9 15.0 %copy-start.5 = (s32[1,64,64]{2,1,0:T(8,128)S(1)}, s32[1,64,64]{2,1,0:T(8,128)}, u32[]{:S(2)}) copy-start(s32[1,64,64]{2,1,0:T(8,128)} %param.20) | copy-start | bytes 49156
  41.9 15.0 %copy-start.6 = (s32[1,64,64]{2,1,0:T(8,128)S(1)}, s32[1,64,64]{2,1,0:T(8,128)}, u32[]{:S(2)}) copy-start(s32[1,64,64]{2,1,0:T(8,128)} %param.19) | copy-start | bytes 49156
  41.9 15.2 %copy-start.4 = (f32[32,2048]{1,0:T(8,128)S(1)}, f32[32,2048]{1,0:T(8,128)}, u32[]{:S(2)}) copy-start(f32[32,2048]{1,0:T(8,128)} %param.13) | copy-start | bytes 786436
  41.9 15.6 %copy-start.1 = (f32[2048]{0:T(1024)S(1)}, f32[2048]{0:T(1024)}, u32[]{:S(2)}) copy-start(f32[2048]{0:T(1024)} %param.14) | copy-start | bytes 24580
  43.4 51.3 %all-to-all-start = ((f32[64,1,2048]{2,1,0:T(1,128)}), f32[64,1,2048]{2,1,0:T(1,128)}, u32[]{:S(2)}, u32[]{:S(2)}) async-start(f32[64,1,2048]{2,1,0:T(1,128)} %reshape.235), calls=%async_computation | async-start | bytes 1048576 | tf_op jit(solution)/shard_map/all_to_all | solution.py:91
  150.8 22.2 %all-to-all-start.1 = ((bf16[64,2,1024]{2,1,0:T(2,128)(2,1)}), bf16[64,2,1024]{2,1,0:T(2,128)(2,1)S(1)}, u32[]{:S(2)}, u32[]{:S(2)}) async-start(bf16[64,2,1024]{2,1,0:T(2,128)(2,1)} %reshape.237), calls=%async_computation.1 | async-start | bytes 524288 | tf_op jit(solution)/shard_map/all_to_all | solution.py:99
  161.1 74.9 %all-gather.3.cloned.1.call-start = ((), (), s32[]{:S(2)}) async-start(), calls=%async_computation.6 | async-start | bytes 1179648 | tf_op jit(solution)/shard_map/all_gather | solution.py:127
  186.6 6.0 %copy-start.15 = (s32[4]{0:T(128)S(1)}, s32[4]{0:T(128)}, u32[]{:S(2)}) copy-start(s32[4]{0:T(128)} %copy-done.14) | copy-start | bytes 52
  186.6 9.7 %copy-start.13 = (s32[4]{0:T(128)S(1)}, s32[4]{0:T(128)}, u32[]{:S(2)}) copy-start(s32[4]{0:T(128)} %copy-done.12) | copy-start | bytes 52
  187.1 49.0 %copy-start.2 = (bf16[256,2048]{1,0:T(8,128)(2,1)S(1)}, bf16[256,2048]{1,0:T(8,128)(2,1)}, u32[]{:S(2)}) copy-start(bf16[256,2048]{1,0:T(8,128)(2,1)} %param.21) | copy-start | bytes 3145732
  188.2 4.4 collective-permute-start.2
  190.7 5.6 %collective-permute-start.3 = (f32[32,4,128]{2,1,0:T(4,128)S(1)}, f32[32,4,128]{2,1,0:T(4,128)S(1)}, u32[]{:S(2)}, u32[]{:S(2)}) collective-permute-start(f32[32,4,128]{2,1,0:T(4,128)S(1)} %get-tuple-element.9), channel_id=1, source_target_pairs={{0,8},{8,16},{16,24},{24,32},{32,40},{40,48},{48,56},{56,64},{64,7... | collective-permute-start | bytes 196616 | tf_op jit(solution)/shard_map/ppermute | solution.py:23
  197.4 246.7 %all-gather.5.cloned.1.call-start = ((), (), s32[]{:S(2)}) async-start(), calls=%async_computation.7 | async-start | bytes 1179648 | tf_op jit(solution)/shard_map/all_gather | solution.py:127
  252.2 9.5 %copy-start.10 = (pred[16,4]{1,0:T(8,128)(4,1)S(1)}, pred[16,4]{1,0:T(8,128)(4,1)}, u32[]{:S(2)}) copy-start(pred[16,4]{1,0:T(8,128)(4,1)} %copy-done.9) | copy-start | bytes 196
  253.7 4.4 collective-permute-start.5
  255.7 5.2 %collective-permute-start.4 = (bf16[32,4,128]{2,1,0:T(4,128)(2,1)S(1)}, bf16[32,4,128]{2,1,0:T(4,128)(2,1)S(1)}, u32[]{:S(2)}, u32[]{:S(2)}) collective-permute-start(bf16[32,4,128]{2,1,0:T(4,128)(2,1)S(1)} %fusion.8), channel_id=1, source_target_pairs={{0,8},{8,16},{16,24},{24,32},{32,40},{40,48},{48,56},{56,64},{64,7... | collective-permute-start | bytes 98312 | tf_op jit(solution)/shard_map/ppermute | solution.py:23
  264.5 14.1 %copy-start.8 = (pred[4096]{0:T(1024)(128)(4,1)S(1)}, pred[4096]{0:T(1024)(128)(4,1)}, u32[]{:S(2)}) copy-start(pred[4096]{0:T(1024)(128)(4,1)} %copy-done.7) | copy-start | bytes 12292
  393.5 50.6 %copy-start.3 = (bf16[256,2048]{1,0:T(8,128)(2,1)S(1)}, bf16[256,2048]{1,0:T(8,128)(2,1)}, u32[]{:S(2)}) copy-start(bf16[256,2048]{1,0:T(8,128)(2,1)} %param.21) | copy-start | bytes 3145732
  394.6 4.4 collective-permute-start.6
  397.1 5.6 %collective-permute-start.7 = (f32[32,4,128]{2,1,0:T(4,128)S(1)}, f32[32,4,128]{2,1,0:T(4,128)S(1)}, u32[]{:S(2)}, u32[]{:S(2)}) collective-permute-start(f32[32,4,128]{2,1,0:T(4,128)S(1)} %get-tuple-element.6), channel_id=1, source_target_pairs={{0,8},{8,16},{16,24},{24,32},{32,40},{40,48},{48,56},{56,64},{64,7... | collective-permute-start | bytes 196616 | tf_op jit(solution)/shard_map/ppermute | solution.py:23
Sparse Core Ops, SparseCore 0:
  197.5 38.4 all-gather.2
  404.0 40.1 all-gather.4
where the time goes:
time: 470 us; the launch traced here: 468 us
  blocking collectives  138 us (29%)
  local copies, waits for them, and re-layouts  123 us (26%)
  waiting for transfers between devices  99.7 us (21%)
  starting transfers between devices  41.4 us (9%)
  other arithmetic  40.2 us (9%)
  between operations  14.1 us (3%)
  matrix products  11.5 us (2%)
    all_gather x2, waiting for transfers between devices, on_device(): lax.all_gather(flat_grad, 'snap', axis=0, tiled=True)  78.9 us
    psum x2, blocking collectives, snapshot_total(): return lax.psum(partial_sum, 'snap')  63 us
    all_to_all x2, blocking collectives, on_device(): lax.all_to_all(rows_all, 'snap', split_axis=0, concat_axis=1, tiled=True)  28.8 us
    all_to_all x1, blocking collectives, on_device(): lax.all_to_all(outgoing, 'area', split_axis=1, concat_axis=1, tiled=True)  28.7 us
    gather x2, local copies, waits for them, and re-layouts, on_device(): jnp.take(predicted, own_gather, axis=1)  28.2 us
    gather x1, local copies, waits for them, and re-layouts, on_device(): collector_variance = jnp.take(reading_error_spread, hub_pickup)  23 us
    scatter x2, local copies, waits for them, and re-layouts, on_device(): weighted = jnp.zeros((snap_dev, READING_LINES), jnp.bfloat16).at[:, own_p...  22.5 us
    all_to_all x1, blocking collectives, on_device(): lax.all_to_all(scaled, 'area', split_axis=1, concat_axis=1, tiled=True)  17.6 us
  transfers between devices with their start and end apart: 12, of which 6 were waited for; matrix products, arithmetic and copies ran while one was open for 9% of the time, Pallas kernels for 0%

commit v1 on v0

v1 whole, which is shorter than its diff:
```python
import functools

import jax
import jax.numpy as jnp
from jax import lax
from jax.experimental import pallas as pl
from jax.experimental.pallas import tpu as pltpu
from jax.sharding import PartitionSpec as P

ITERS = 2
LANES = 128
MESH = pl.DeviceIdType.MESH
NT = (((1,), (1,)), ((), ()))


def step_kernel(
    dims,
    z_ref,
    var_ref,
    x_ref,
    tiles_hbm,
    pos_ref,
    ties_ref,
    holder_ref,
    hub_ref,
    gain_hbm,
    out_ref,
    tiles,
    gain,
    gain_t,
    tile_index,
    table,
    zs,
    zr,
    vs,
    vr,
    arrived,
    inv_q,
    inv_lane,
    z_own,
    v_own,
    aug,
    fs,
    fr,
    resid,
    ssr,
    wgt,
    grads,
    bs,
    br,
    gath,
    us,
    ur,
    local_sem,
    z_send,
    z_recv,
    v_send,
    v_recv,
    f_send,
    f_recv,
    s_send,
    s_recv,
    b_send,
    b_recv,
    ring_send,
    ring_recv,
    u_send,
    u_recv,
):
    areas, peers, snaps, nb, mb, touched, ties, cap = dims
    half = snaps // 2
    chunks = areas * cap // LANES
    rows = nb * LANES // peers
    units = nb // 2
    piece_units = 2
    pieces = units // piece_units
    reach = peers // 2
    slots = nb + 2 * ties
    all_tiles = mb * touched
    snaps_all = snaps * peers
    f32, bf16, i32 = jnp.float32, jnp.bfloat16, jnp.int32

    a = lax.axis_index("area")
    s = lax.axis_index("snap")
    has_lower = a > 0
    has_upper = a < areas - 1

    tiles_copy = pltpu.make_async_copy(
        tiles_hbm, tiles.at[pl.ds(0, all_tiles)], local_sem.at[0]
    )
    gain_copy = pltpu.make_async_copy(gain_hbm, gain, local_sem.at[1])
    tiles_copy.start()
    gain_copy.start()

    barrier = pltpu.get_barrier_semaphore()

    def greet_area(i, carry):
        pl.semaphore_signal(
            barrier, inc=1, device_id=(lax.rem(a + i, areas), s), device_id_type=MESH
        )
        return carry

    def greet_snap(i, carry):
        pl.semaphore_signal(
            barrier, inc=1, device_id=(a, lax.rem(s + i, peers)), device_id_type=MESH
        )
        return carry

    lax.fori_loop(1, areas, greet_area, 0)
    lax.fori_loop(1, peers, greet_snap, 0)

    lane_a = lax.broadcasted_iota(i32, (areas, LANES), 1)
    for index, listing in enumerate((hub_ref, holder_ref)):
        both = jnp.concatenate([listing[...], listing[...]], axis=1)
        table[index] = both
    for block in range(nb):
        aug[block] = x_ref[:, block * LANES : (block + 1) * LANES].astype(bf16)
    aug[slots] = jnp.zeros((snaps, LANES), bf16)
    for step in range(ITERS):
        for side in range(2):
            br[step, side, ties] = jnp.zeros((snaps, LANES), f32)

    @pl.when(jnp.logical_not(has_lower))
    def _():
        for t in range(ties):
            aug[nb + t] = jnp.zeros((snaps, LANES), bf16)
            for step in range(ITERS):
                br[step, 0, t] = jnp.zeros((snaps, LANES), f32)

    @pl.when(jnp.logical_not(has_upper))
    def _():
        for t in range(ties):
            aug[nb + ties + t] = jnp.zeros((snaps, LANES), bf16)
            for step in range(ITERS):
                br[step, 1, t] = jnp.zeros((snaps, LANES), f32)

    pl.semaphore_wait(barrier, areas - 1 + peers - 1)

    def frontier_copy(step, side):
        return pltpu.make_async_remote_copy(
            src_ref=fs.at[step, side],
            dst_ref=fr.at[step, 1 - side],
            send_sem=f_send.at[step, side],
            recv_sem=f_recv.at[step, side],
            device_id=(a - 1 if side == 0 else a + 1, s),
            device_id_type=MESH,
        )

    def frontier_start(step):
        for side in range(2):
            for t in range(ties):
                entry = ties_ref[side, t]
                fs[step, side, t] = aug[jnp.where(entry >= 0, entry, slots)]

        @pl.when(has_lower)
        def _():
            frontier_copy(step, 0).start()

        @pl.when(has_upper)
        def _():
            frontier_copy(step, 1).start()

    def frontier_wait(step):
        @pl.when(has_lower)
        def _():
            frontier_copy(step, 1).wait_recv()
            for t in range(ties):
                aug[nb + t] = fr[step, 0, t]

        @pl.when(has_upper)
        def _():
            frontier_copy(step, 0).wait_recv()
            for t in range(ties):
                aug[nb + ties + t] = fr[step, 1, t]

    frontier_start(0)

    def table_row(index, q):
        even = table[index, pl.ds(2 * q, 1), :]
        odd = table[index, pl.ds(2 * q + 1, 1), :]
        lane = lax.broadcasted_iota(i32, (1, LANES), 1)
        return jnp.where(lane < cap, even, odd)

    lane_h = lax.broadcasted_iota(i32, (half, LANES), 1)

    def route_out(i, carry):
        q = lax.rem(lax.div(a, 2) + i, chunks)
        where_at = table_row(0, q)
        block_of = lax.shift_right_arithmetic(where_at, 7)
        lane_of = where_at & (LANES - 1)
        lanes = jnp.broadcast_to(lane_of, (snaps, LANES))
        from_block = jnp.broadcast_to(block_of, (snaps, LANES))
        taken = jnp.zeros((snaps, LANES), f32)
        for block in range(mb):
            found = jnp.take_along_axis(
                z_ref[:, block * LANES : (block + 1) * LANES], lanes, axis=1
            )
            taken = jnp.where(from_block == block, found, taken)
        low, high = taken[:half], taken[half:]
        zs[2 * q] = jnp.where(lane_h < cap, low, pltpu.roll(high, cap, 1))
        zs[2 * q + 1] = jnp.where(lane_h < cap, pltpu.roll(low, cap, 1), high)
        var_found = jnp.take_along_axis(
            var_ref[...], jnp.broadcast_to(lane_of, (mb, LANES)), axis=1
        )
        var_rows = lax.broadcasted_iota(i32, (mb, LANES), 0)
        vs[q] = jnp.sum(
            jnp.where(var_rows == jnp.broadcast_to(block_of, (mb, LANES)), var_found, 0.0),
            axis=0,
            keepdims=True,
        )
        for parity in range(2):
            d = 2 * q + parity

            @pl.when(d != a)
            def _():
                pltpu.make_async_remote_copy(
                    src_ref=zs.at[d],
                    dst_ref=zr.at[a],
                    send_sem=z_send,
                    recv_sem=z_recv,
                    device_id=(d, s),
                    device_id_type=MESH,
                ).start()
                pltpu.make_async_remote_copy(
                    src_ref=vs.at[q],
                    dst_ref=vr.at[a],
                    send_sem=v_send,
                    recv_sem=v_recv,
                    device_id=(d, s),
                    device_id_type=MESH,
                ).start()

            @pl.when(d == a)
            def _():
                pltpu.make_async_copy(zs.at[d], zr.at[a], z_recv).start()
                pltpu.make_async_copy(vs.at[q], vr.at[a], v_recv).start()

        return carry

    lax.fori_loop(0, chunks, route_out, 0)

    sub_q = lax.broadcasted_iota(i32, (mb, LANES), 0)
    lane_q = lax.broadcasted_iota(i32, (mb, LANES), 1)
    sub_l = lax.broadcasted_iota(i32, (LANES, LANES), 0)

    def invert(q, total):
        where_at = table_row(1, q)
        mine = jnp.broadcast_to(lax.shift_right_arithmetic(where_at, 7), (mb, LANES)) == sub_q
        left = jnp.concatenate(
            [jnp.where(mine, lane_q, 0).astype(f32), jnp.where(mine, q, 0).astype(f32)], axis=0
        ).astype(bf16)
        hit = jnp.broadcast_to(where_at & (LANES - 1), (LANES, LANES)) == sub_l
        right = jnp.where(hit, 1.0, 0.0).astype(bf16)
        return total + lax.dot_general(left, right, NT, preferred_element_type=f32)

    inverse = lax.fori_loop(0, chunks, invert, jnp.zeros((2 * mb, LANES), f32))
    inv_lane[...] = inverse[:mb].astype(i32) & (LANES - 1)
    inv_q[...] = inverse[mb:].astype(i32)

    def index_tiles(n, carry):
        for j in range(mb):
            which = all_tiles
            for k in range(touched):
                tile = j * touched + k
                which = jnp.where(pos_ref[j, k] == n, tile, which)
            tile_index[n, j] = which
        return carry

    lax.fori_loop(0, slots, index_tiles, 0)
    tiles[all_tiles] = jnp.zeros((LANES, LANES), bf16)

    gain_copy.wait()
    gain_t[...] = gain[...].T
    tiles_copy.wait()

    def predict(step):
        frontier_wait(step)

        def body(j, carry):
            total = jnp.zeros((snaps, LANES), f32)
            for k in range(touched):
                total += lax.dot_general(
                    aug[pos_ref[j, k]],
                    tiles[j * touched + k],
                    NT,
                    preferred_element_type=f32,
                )
            resid[j] = total
            return carry

        lax.fori_loop(0, mb, body, 0, unroll=2)

    predict(0)

    pltpu.make_async_copy(zr, zr, z_recv).wait()
    pltpu.make_async_copy(vr, vr, v_recv).wait()

    def unpack(q, carry):
        even, odd = zr[2 * q], zr[2 * q + 1]
        arrived[q, pl.ds(0, half)] = jnp.where(lane_h < cap, even, pltpu.roll(odd, cap, 1))
        arrived[q, pl.ds(half, half)] = jnp.where(lane_h < cap, pltpu.roll(even, cap, 1), odd)
        return carry

    lax.fori_loop(0, chunks, unpack, 0, unroll=2)
    variances = jnp.concatenate([vr[c] for c in range(areas)], axis=0)
    sub_a = lax.broadcasted_iota(i32, (areas, LANES), 0)
    my_half = lax.rem(a, 2) * cap

    def reorder(j, carry):
        lane_of = inv_lane[pl.ds(j, 1), :]
        chunk_of = inv_q[pl.ds(j, 1), :]
        lanes = jnp.broadcast_to(lane_of, (snaps, LANES))
        from_chunk = jnp.broadcast_to(chunk_of, (snaps, LANES))
        taken = jnp.zeros((snaps, LANES), f32)
        for q in range(chunks):
            found = jnp.take_along_axis(arrived[q], lanes, axis=1)
            taken = jnp.where(from_chunk == q, found, taken)
        z_own[j] = taken
        hub = 2 * chunk_of + lax.shift_right_arithmetic(lane_of, 6)
        lane_v = (lane_of & (cap - 1)) + my_half
        found = jnp.take_along_axis(
            variances, jnp.broadcast_to(lane_v, (areas, LANES)), axis=1
        )
        v_own[pl.ds(j, 1), :] = jnp.sum(
            jnp.where(jnp.broadcast_to(hub, (areas, LANES)) == sub_a, found, 0.0),
            axis=0,
            keepdims=True,
        )
        return carry

    lax.fori_loop(0, mb, reorder, 0)

    def spread_copy(step, i):
        peer = lax.rem(s + i, peers)
        return pltpu.make_async_remote_copy(
            src_ref=ssr.at[step, s],
            dst_ref=ssr.at[step, s],
            send_sem=s_send.at[step, i],
            recv_sem=s_recv.at[step, s],
            device_id=(a, peer),
            device_id_type=MESH,
        )

    def spread_wait(step, i):
        source = lax.rem(s + i, peers)
        pltpu.make_async_remote_copy(
            src_ref=ssr.at[step, source],
            dst_ref=ssr.at[step, source],
            send_sem=s_send.at[step, i],
            recv_sem=s_recv.at[step, source],
            device_id=(a, source),
            device_id_type=MESH,
        ).wait_recv()

    def boundary_copy(step, side):
        return pltpu.make_async_remote_copy(
            src_ref=bs.at[step, side],
            dst_ref=br.at[step, 1 - side, pl.ds(0, ties)],
            send_sem=b_send.at[step, side],
            recv_sem=b_recv.at[step, side],
            device_id=(a - 1 if side == 0 else a + 1, s),
            device_id_type=MESH,
        )

    def ring_copy(step, way, hop, piece, chunk):
        beside = lax.rem(s + 1, peers) if way == 0 else lax.rem(s + peers - 1, peers)
        part = pl.ds(piece * piece_units, piece_units)
        return pltpu.make_async_remote_copy(
            src_ref=gath.at[step, chunk, part],
            dst_ref=gath.at[step, chunk, part],
            send_sem=ring_send.at[step, way, hop - 1, piece],
            recv_sem=ring_recv.at[step, way, hop - 1, piece],
            device_id=(a, beside),
            device_id_type=MESH,
        )

    def ring_pieces(way, hop):
        if hop < reach:
            return range(pieces)
        return range(pieces // 2) if way == 0 else range(pieces // 2, pieces)

    def came_from(way, hop):
        return lax.rem(s + peers - hop, peers) if way == 0 else lax.rem(s + hop, peers)

    def update_copy(step, chunk):
        return pltpu.make_async_remote_copy(
            src_ref=us.at[step, chunk],
            dst_ref=ur.at[step, s],
            send_sem=u_send.at[step, chunk],
            recv_sem=u_recv.at[step, s],
            device_id=(a, chunk),
            device_id_type=MESH,
        )

    def slot_pair(n2):
        total = jnp.zeros((snaps, 2 * LANES), f32)
        for jp in range(mb // 2):
            left = [tiles[tile_index[2 * n2, 2 * jp + r]] for r in range(2)]
            right = [tiles[tile_index[2 * n2 + 1, 2 * jp + r]] for r in range(2)]
            weights = jnp.concatenate(
                [jnp.concatenate(left, axis=0), jnp.concatenate(right, axis=0)], axis=1
            )
            total += jnp.dot(wgt[jp], weights, preferred_element_type=f32)
        return total

    def gain_piece(step, chunk, piece):
        total = jnp.zeros((snaps, rows), f32)
        for u in range(piece * piece_units, (piece + 1) * piece_units):
            total += jnp.dot(
                gath[step, chunk, u],
                gain_t[u * 2 * LANES : (u + 1) * 2 * LANES, :],
                preferred_element_type=f32,
            )
        return total

    for step in range(ITERS):
        if step > 0:
            frontier_start(step)
            predict(step)

        for j in range(mb):
            left_over = z_own[j] - resid[j]
            resid[j] = left_over
            ssr[step, s, pl.ds(j, 1), :] = jnp.sum(
                left_over * left_over, axis=0, keepdims=True
            )
        for i in range(1, peers):
            spread_copy(step, i).start()
        for i in range(1, peers):
            spread_wait(step, i)
        total = ssr[step, 0]
        for i in range(1, peers):
            total += ssr[step, i]
        scale = v_own[...] + total / snaps_all
        for j in range(mb):
            wgt[j // 2, :, (j % 2) * LANES : (j % 2 + 1) * LANES] = (
                resid[j] / scale[j : j + 1, :]
            ).astype(bf16)

        def outer_slots(i, carry):
            pair = slot_pair(nb // 2 + i)
            side, first = lax.div(i, ties // 2), lax.rem(i, ties // 2) * 2
            bs[step, side, first] = pair[:, :LANES]
            bs[step, side, first + 1] = pair[:, LANES:]
            return carry

        lax.fori_loop(0, ties, outer_slots, 0)

        @pl.when(has_lower)
        def _():
            boundary_copy(step, 0).start()

        @pl.when(has_upper)
        def _():
            boundary_copy(step, 1).start()

        def own_slots(n2, carry):
            pair = slot_pair(n2)
            grads[2 * n2] = pair[:, :LANES]
            grads[2 * n2 + 1] = pair[:, LANES:]
            return carry

        lax.fori_loop(0, nb // 2, own_slots, 0)

        @pl.when(has_upper)
        def _():
            boundary_copy(step, 0).wait_recv()

        @pl.when(has_lower)
        def _():
            boundary_copy(step, 1).wait_recv()

        for block in range(nb):
            total = grads[block]
            for side in range(2):
                which = ties
                for t in range(ties):
                    which = jnp.where(ties_ref[side, t] == block, t, which)
                total += br[step, side, which]
            gath[step, s, block // 2, :, (block % 2) * LANES : (block % 2 + 1) * LANES] = (
                total.astype(bf16)
            )
            if block % (2 * piece_units) == 2 * piece_units - 1:
                for way in range(2):
                    ring_copy(step, way, 1, block // (2 * piece_units), s).start()

        own = gain_piece(step, s, 0)
        for piece in range(1, pieces):
            own += gain_piece(step, s, piece)
        ur[step, s] = own

        for hop in range(1, reach + 1):
            sums = [None, None]
            for turn in range(len(ring_pieces(0, hop))):
                for way in range(2):
                    piece = ring_pieces(way, hop)[turn]
                    chunk = came_from(way, hop)
                    ring_copy(step, way, hop, piece, chunk).wait_recv()
                    if hop < reach and piece in ring_pieces(way, hop + 1):
                        ring_copy(step, way, hop + 1, piece, chunk).start()
                for way in range(2):
                    piece = ring_pieces(way, hop)[turn]
                    part = gain_piece(step, came_from(way, hop), piece)
                    sums[way] = part if sums[way] is None else sums[way] + part
            if hop < reach:
                for way in range(2):
                    us[step, came_from(way, hop)] = sums[way]
                    update_copy(step, came_from(way, hop)).start()
            else:
                us[step, came_from(0, hop)] = sums[0] + sums[1]
                update_copy(step, came_from(0, hop)).start()

        before = x_ref if step == 0 else out_ref
        for i in range(peers):

            @pl.when(i != s)
            def _():
                pltpu.make_async_remote_copy(
                    src_ref=us.at[step, i],
                    dst_ref=ur.at[step, i],
                    send_sem=u_send.at[step, i],
                    recv_sem=u_recv.at[step, i],
                    device_id=(a, i),
                    device_id_type=MESH,
                ).wait_recv()

        for i in range(peers):
            cols = slice(i * rows, (i + 1) * rows)
            after = before[:, cols] + ur[step, i]
            out_ref[:, cols] = after
            if step + 1 < ITERS:
                for r in range(rows // LANES):
                    aug[i * (rows // LANES) + r] = after[
                        :, r * LANES : (r + 1) * LANES
                    ].astype(bf16)

    pltpu.make_async_copy(
        zs.at[pl.ds(0, areas - 1)], zr.at[pl.ds(0, areas - 1)], z_send
    ).wait()
    pltpu.make_async_copy(
        vr.at[pl.ds(0, areas - 1)], vr.at[pl.ds(0, areas - 1)], v_send
    ).wait()
    for step in range(ITERS):

        @pl.when(has_lower)
        def _():
            frontier_copy(step, 0).wait_send()
            boundary_copy(step, 0).wait_send()

        @pl.when(has_upper)
        def _():
            frontier_copy(step, 1).wait_send()
            boundary_copy(step, 1).wait_send()

        for i in range(1, peers):
            spread_copy(step, i).wait_send()
            update_copy(step, lax.rem(s + i, peers)).wait_send()
        for way in range(2):
            for hop in range(1, reach + 1):
                for piece in ring_pieces(way, hop):
                    ring_copy(step, way, hop, piece, s).wait_send()


def on_device(
    phasor_readings,
    reading_error_spread,
    starting_voltages,
    derivative_pieces,
    derivative_tile_position,
    frontier_voltage_pieces,
    holder_line_order,
    hub_line_order,
    reciprocal_normal_operator,
):
    areas, peers = lax.axis_size("area"), lax.axis_size("snap")
    snaps, states = starting_voltages.shape
    nb = states // LANES
    mb, touched = derivative_tile_position.shape[1:]
    ties = frontier_voltage_pieces.shape[2]
    cap = holder_line_order.shape[2]
    rows = states // peers
    chunks = areas * cap // LANES
    slots = nb + 2 * ties
    all_tiles = mb * touched
    units = nb // 2
    reach = peers // 2
    pieces = units // 2
    f32, bf16, i32 = jnp.float32, jnp.bfloat16, jnp.int32
    vmem = pl.BlockSpec(memory_space=pltpu.VMEM)
    smem = pl.BlockSpec(memory_space=pltpu.SMEM)
    hbm = pl.BlockSpec(memory_space=pltpu.HBM)
    dma = pltpu.SemaphoreType.DMA
    dims = (areas, peers, snaps, nb, mb, touched, ties, cap)
    return pl.pallas_call(
        functools.partial(step_kernel, dims),
        out_shape=jax.ShapeDtypeStruct((snaps, states), f32),
        in_specs=[vmem, vmem, vmem, hbm, smem, smem, vmem, vmem, hbm],
        out_specs=vmem,
        scratch_shapes=[
            pltpu.VMEM((all_tiles + 1, LANES, LANES), bf16),
            pltpu.VMEM((rows, states), bf16),
            pltpu.VMEM((states, rows), bf16),
            pltpu.SMEM((slots, mb), i32),
            pltpu.VMEM((2, areas, LANES), i32),
            pltpu.VMEM((areas, snaps // 2, LANES), f32),
            pltpu.VMEM((areas, snaps // 2, LANES), f32),
            pltpu.VMEM((chunks, 1, LANES), f32),
            pltpu.VMEM((areas, 1, LANES), f32),
            pltpu.VMEM((chunks, snaps, LANES), f32),
            pltpu.VMEM((mb, LANES), i32),
            pltpu.VMEM((mb, LANES), i32),
            pltpu.VMEM((mb, snaps, LANES), f32),
            pltpu.VMEM((mb, LANES), f32),
            pltpu.VMEM((slots + 1, snaps, LANES), bf16),
            pltpu.VMEM((ITERS, 2, ties, snaps, LANES), bf16),
            pltpu.VMEM((ITERS, 2, ties, snaps, LANES), bf16),
            pltpu.VMEM((mb, snaps, LANES), f32),
            pltpu.VMEM((ITERS, peers, mb, LANES), f32),
            pltpu.VMEM((mb // 2, snaps, 2 * LANES), bf16),
            pltpu.VMEM((nb, snaps, LANES), f32),
            pltpu.VMEM((ITERS, 2, ties, snaps, LANES), f32),
            pltpu.VMEM((ITERS, 2, ties + 1, snaps, LANES), f32),
            pltpu.VMEM((ITERS, peers, units, snaps, 2 * LANES), bf16),
            pltpu.VMEM((ITERS, peers, snaps, rows), f32),
            pltpu.VMEM((ITERS, peers, snaps, rows), f32),
            dma((2,)),
            dma(()),
            dma(()),
            dma(()),
            dma(()),
            dma((ITERS, 2)),
            dma((ITERS, 2)),
            dma((ITERS, peers)),
            dma((ITERS, peers)),
            dma((ITERS, 2)),
            dma((ITERS, 2)),
            dma((ITERS, 2, reach, pieces)),
            dma((ITERS, 2, reach, pieces)),
            dma((ITERS, peers)),
            dma((ITERS, peers)),
        ],
        compiler_params=pltpu.CompilerParams(collective_id=0, has_side_effects=True),
        name="estimate",
    )(
        phasor_readings,
        reading_error_spread.reshape(mb, LANES),
        starting_voltages,
        derivative_pieces.reshape(all_tiles, LANES, LANES),
        derivative_tile_position[0],
        frontier_voltage_pieces[0],
        holder_line_order[0],
        hub_line_order[0],
        reciprocal_normal_operator,
    )


def solution(mesh):
    placed = (
        P("snap", "area"),
        P("area"),
        P("snap", "area"),
        P("area", None, None, None),
        P("area", None, None),
        P("area", None, None),
        P("area", None, None),
        P("area", None, None),
        P(("area", "snap"), None),
    )
    return jax.shard_map(
        on_device, mesh=mesh, in_specs=placed, out_specs=P("snap", "area"), check_vma=False
    )
```

time: 470 us -> 113 us (0.24)
  the two profiles are of different devices: /device:TPU:4 before, /device:TPU:8 now
where the time goes in v1:
time: 113 us
  Pallas kernels  109 us (96%)
  local copies, waits for them, and re-layouts  3.03 us (3%)
    pallas_call x1, Pallas kernels, on_device(): pl.pallas_call(functools.partial(step_kernel, dims), out_shape=jax.ShapeD...  109 us

profile of v1, /device:TPU:8, one launch (start us, length us, event | category | flops | bytes accessed | tf_op | source)
XLA Modules:
  0.0 112.5 jit_solution(8012047296101775721)
XLA Ops:
  0.0 1.4 %copy.10.pos_ref = s32[16,4]{1,0:T(8,128)} copy(s32[16,4]{0,1:T(4,128)} %bitcast.10) | data formatting | bytes 512 | tf_op jit(solution)/shard_map/squeeze | solution.py:649
  1.4 109.5 %estimate.1 = f32[32,2048]{1,0:T(8,128)} custom-call(f32[32,2048]{1,0:T(8,128)} %z_ref.1, f32[16,128]{1,0:T(8,128)} %bitcast.9, f32[32,2048]{1,0:T(8,128)} %x_ref.1, bf16[64,128,128]{2,1,0:T(8,128)(2,1)} %bitcast.6, s32[16,4]{1,0:T(8,128)} %copy.10.pos_ref, s32[2,4]{1,0:T(2,128)} %bitcast.11, s32[64,64]{1,0:T(8,128)} %bitcast.7, s32[64,64]{1,0:T(8,128)} %bitcast.8, ...), custom_call_target="tpu_custom_call" | custom-call | tf_op jit(solution)/shard_map/estimate/pallas_call | solution.py:594
  110.9 1.7 %copy.12 = f32[32,2048]{1,0:T(8,128)} copy(f32[32,2048]{1,0:T(8,128)} %estimate.1) | data formatting | bytes 524288

commit v2 on v1

--- a/solution.py
+++ b/solution.py
@@ -8,6 +8,7 @@
 from jax.sharding import PartitionSpec as P
 
 ITERS = 2
+UNROLL = (8, 8, 4, 4, 4)
 LANES = 128
 MESH = pl.DeviceIdType.MESH
 NT = (((1,), (1,)), ((), ()))
@@ -183,8 +184,16 @@
 
     lane_h = lax.broadcasted_iota(i32, (half, LANES), 1)
 
+    wide = min(chunks, 4)
+    tall = chunks // wide
+
     def route_out(i, carry):
-        q = lax.rem(lax.div(a, 2) + i, chunks)
+        k = lax.rem(i, tall)
+        turn = (k + 1) // 2
+        dy = tall // 2 + turn * (1 - 2 * (k % 2))
+        dx = lax.rem(wide // 2 + lax.div(i, tall), wide)
+        chip = lax.div(a, 2)
+        q = lax.rem(lax.div(chip, wide) + dy, tall) * wide + lax.rem(lax.rem(chip, wide) + dx, wide)
         where_at = table_row(0, q)
         block_of = lax.shift_right_arithmetic(where_at, 7)
         lane_of = where_at & (LANES - 1)
@@ -237,7 +246,7 @@
 
         return carry
 
-    lax.fori_loop(0, chunks, route_out, 0)
+    lax.fori_loop(0, chunks, route_out, 0, unroll=UNROLL[2])
 
     sub_q = lax.broadcasted_iota(i32, (mb, LANES), 0)
     lane_q = lax.broadcasted_iota(i32, (mb, LANES), 1)
@@ -253,7 +262,9 @@
         right = jnp.where(hit, 1.0, 0.0).astype(bf16)
         return total + lax.dot_general(left, right, NT, preferred_element_type=f32)
 
-    inverse = lax.fori_loop(0, chunks, invert, jnp.zeros((2 * mb, LANES), f32))
+    inverse = lax.fori_loop(
+        0, chunks, invert, jnp.zeros((2 * mb, LANES), f32), unroll=UNROLL[0]
+    )
     inv_lane[...] = inverse[:mb].astype(i32) & (LANES - 1)
     inv_q[...] = inverse[mb:].astype(i32)
 
@@ -262,15 +273,10 @@
             which = all_tiles
             for k in range(touched):
                 tile = j * touched + k
-                which = jnp.where(pos_ref[j, k] == n, tile, which)
+                which = jnp.where(pos_ref[k, j] == n, tile, which)
             tile_index[n, j] = which
         return carry
 
-    lax.fori_loop(0, slots, index_tiles, 0)
-    tiles[all_tiles] = jnp.zeros((LANES, LANES), bf16)
-
-    gain_copy.wait()
-    gain_t[...] = gain[...].T
     tiles_copy.wait()
 
     def predict(step):
@@ -280,7 +286,7 @@
             total = jnp.zeros((snaps, LANES), f32)
             for k in range(touched):
                 total += lax.dot_general(
-                    aug[pos_ref[j, k]],
+                    aug[pos_ref[k, j]],
                     tiles[j * touched + k],
                     NT,
                     preferred_element_type=f32,
@@ -288,7 +294,7 @@
             resid[j] = total
             return carry
 
-        lax.fori_loop(0, mb, body, 0, unroll=2)
+        lax.fori_loop(0, mb, body, 0, unroll=min(mb, UNROLL[1]))
 
     predict(0)
 
@@ -301,7 +307,7 @@
         arrived[q, pl.ds(half, half)] = jnp.where(lane_h < cap, pltpu.roll(even, cap, 1), odd)
         return carry
 
-    lax.fori_loop(0, chunks, unpack, 0, unroll=2)
+    lax.fori_loop(0, chunks, unpack, 0, unroll=4)
     variances = jnp.concatenate([vr[c] for c in range(areas)], axis=0)
     sub_a = lax.broadcasted_iota(i32, (areas, LANES), 0)
     my_half = lax.rem(a, 2) * cap
@@ -328,7 +334,7 @@
         )
         return carry
 
-    lax.fori_loop(0, mb, reorder, 0)
+    lax.fori_loop(0, mb, reorder, 0, unroll=min(mb, UNROLL[3]))
 
     def spread_copy(step, i):
         peer = lax.rem(s + i, peers)
@@ -352,12 +358,12 @@
             device_id_type=MESH,
         ).wait_recv()
 
-    def boundary_copy(step, side):
+    def boundary_copy(step, side, part):
         return pltpu.make_async_remote_copy(
-            src_ref=bs.at[step, side],
-            dst_ref=br.at[step, 1 - side, pl.ds(0, ties)],
-            send_sem=b_send.at[step, side],
-            recv_sem=b_recv.at[step, side],
+            src_ref=bs.at[step, side, pl.ds(2 * part, 2)],
+            dst_ref=br.at[step, 1 - side, pl.ds(2 * part, 2)],
+            send_sem=b_send.at[step, side, part],
+            recv_sem=b_recv.at[step, side, part],
             device_id=(a - 1 if side == 0 else a + 1, s),
             device_id_type=MESH,
         )
@@ -426,6 +432,11 @@
             )
         for i in range(1, peers):
             spread_copy(step, i).start()
+        if step == 0:
+            lax.fori_loop(0, slots, index_tiles, 0)
+            tiles[all_tiles] = jnp.zeros((LANES, LANES), bf16)
+            gain_copy.wait()
+            gain_t[...] = gain[...].T
         for i in range(1, peers):
             spread_wait(step, i)
         total = ssr[step, 0]
@@ -437,22 +448,15 @@
                 resid[j] / scale[j : j + 1, :]
             ).astype(bf16)
 
-        def outer_slots(i, carry):
-            pair = slot_pair(nb // 2 + i)
-            side, first = lax.div(i, ties // 2), lax.rem(i, ties // 2) * 2
-            bs[step, side, first] = pair[:, :LANES]
-            bs[step, side, first + 1] = pair[:, LANES:]
-            return carry
-
-        lax.fori_loop(0, ties, outer_slots, 0)
-
-        @pl.when(has_lower)
-        def _():
-            boundary_copy(step, 0).start()
-
-        @pl.when(has_upper)
-        def _():
-            boundary_copy(step, 1).start()
+        for side in range(2):
+            for part in range(ties // 2):
+                pair = slot_pair(nb // 2 + side * (ties // 2) + part)
+                bs[step, side, 2 * part] = pair[:, :LANES]
+                bs[step, side, 2 * part + 1] = pair[:, LANES:]
+
+                @pl.when(has_lower if side == 0 else has_upper)
+                def _():
+                    boundary_copy(step, side, part).start()
 
         def own_slots(n2, carry):
             pair = slot_pair(n2)
@@ -460,15 +464,17 @@
             grads[2 * n2 + 1] = pair[:, LANES:]
             return carry
 
-        lax.fori_loop(0, nb // 2, own_slots, 0)
+        lax.fori_loop(0, nb // 2, own_slots, 0, unroll=min(nb // 2, UNROLL[4]))
 
         @pl.when(has_upper)
         def _():
-            boundary_copy(step, 0).wait_recv()
+            for part in range(ties // 2):
+                boundary_copy(step, 0, part).wait_recv()
 
         @pl.when(has_lower)
         def _():
-            boundary_copy(step, 1).wait_recv()
+            for part in range(ties // 2):
+                boundary_copy(step, 1, part).wait_recv()
 
         for block in range(nb):
             total = grads[block]
@@ -487,7 +493,7 @@
         own = gain_piece(step, s, 0)
         for piece in range(1, pieces):
             own += gain_piece(step, s, piece)
-        ur[step, s] = own
+        ur[step, s] = own.astype(bf16)
 
         for hop in range(1, reach + 1):
             sums = [None, None]
@@ -504,10 +510,10 @@
                     sums[way] = part if sums[way] is None else sums[way] + part
             if hop < reach:
                 for way in range(2):
-                    us[step, came_from(way, hop)] = sums[way]
+                    us[step, came_from(way, hop)] = sums[way].astype(bf16)
                     update_copy(step, came_from(way, hop)).start()
             else:
-                us[step, came_from(0, hop)] = sums[0] + sums[1]
+                us[step, came_from(0, hop)] = (sums[0] + sums[1]).astype(bf16)
                 update_copy(step, came_from(0, hop)).start()
 
         before = x_ref if step == 0 else out_ref
@@ -526,7 +532,7 @@
 
         for i in range(peers):
             cols = slice(i * rows, (i + 1) * rows)
-            after = before[:, cols] + ur[step, i]
+            after = before[:, cols] + ur[step, i].astype(f32)
             out_ref[:, cols] = after
             if step + 1 < ITERS:
                 for r in range(rows // LANES):
@@ -545,12 +551,14 @@
         @pl.when(has_lower)
         def _():
             frontier_copy(step, 0).wait_send()
-            boundary_copy(step, 0).wait_send()
+            for part in range(ties // 2):
+                boundary_copy(step, 0, part).wait_send()
 
         @pl.when(has_upper)
         def _():
             frontier_copy(step, 1).wait_send()
-            boundary_copy(step, 1).wait_send()
+            for part in range(ties // 2):
+                boundary_copy(step, 1, part).wait_send()
 
         for i in range(1, peers):
             spread_copy(step, i).wait_send()
@@ -621,8 +629,8 @@
             pltpu.VMEM((ITERS, 2, ties, snaps, LANES), f32),
             pltpu.VMEM((ITERS, 2, ties + 1, snaps, LANES), f32),
             pltpu.VMEM((ITERS, peers, units, snaps, 2 * LANES), bf16),
-            pltpu.VMEM((ITERS, peers, snaps, rows), f32),
-            pltpu.VMEM((ITERS, peers, snaps, rows), f32),
+            pltpu.VMEM((ITERS, peers, snaps, rows), bf16),
+            pltpu.VMEM((ITERS, peers, snaps, rows), bf16),
             dma((2,)),
             dma(()),
             dma(()),
@@ -632,8 +640,8 @@
             dma((ITERS, 2)),
             dma((ITERS, peers)),
             dma((ITERS, peers)),
-            dma((ITERS, 2)),
-            dma((ITERS, 2)),
+            dma((ITERS, 2, ties // 2)),
+            dma((ITERS, 2, ties // 2)),
             dma((ITERS, 2, reach, pieces)),
             dma((ITERS, 2, reach, pieces)),
             dma((ITERS, peers)),
@@ -646,7 +654,7 @@
         reading_error_spread.reshape(mb, LANES),
         starting_voltages,
         derivative_pieces.reshape(all_tiles, LANES, LANES),
-        derivative_tile_position[0],
+        derivative_tile_position[0].T,
         frontier_voltage_pieces[0],
         holder_line_order[0],
         hub_line_order[0],

time: 113 us -> 104 us (0.920)
  Pallas kernels: 109 us -> 102 us
  local copies, waits for them, and re-layouts: 3.03 us -> 1.67 us
    pallas_call x1, Pallas kernels: 109 us -> 102 us  [on_device(): pl.pallas_call(functools.partial(step_kernel, dims), out_shape=jax.ShapeD...]
    squeeze x1 -> x0, local copies, waits for them, and re-layouts: 1.35 us -> none  [on_device(): derivative_tile_position[0]]
where the time goes in v2:
time: 104 us
  Pallas kernels  102 us (98%)
  local copies, waits for them, and re-layouts  1.67 us (2%)
    pallas_call x1, Pallas kernels, on_device(): pl.pallas_call(functools.partial(step_kernel, dims), out_shape=jax.ShapeD...  102 us

profile of v2, /device:TPU:8, one launch (start us, length us, event | category | flops | bytes accessed | tf_op | source)
XLA Modules:
  0.0 103.6 jit_solution(10192918143739366696)
XLA Ops:
  0.0 101.9 %estimate.1 = f32[32,2048]{1,0:T(8,128)} custom-call(f32[32,2048]{1,0:T(8,128)} %z_ref.1, f32[16,128]{1,0:T(8,128)} %bitcast.11, f32[32,2048]{1,0:T(8,128)} %x_ref.1, bf16[64,128,128]{2,1,0:T(8,128)(2,1)} %bitcast.8, s32[4,16]{1,0:T(4,128)} %bitcast.12, s32[2,4]{1,0:T(2,128)} %bitcast.13, s32[64,64]{1,0:T(8,128)} %bitcast.9, s32[64,64]{1,0:T(8,128)} %bitcast.10, ...), custom_call_target="tpu_custom_call" | custom-call | tf_op jit(solution)/shard_map/estimate/pallas_call | solution.py:602
  101.9 1.7 %copy.11 = f32[32,2048]{1,0:T(8,128)} copy(f32[32,2048]{1,0:T(8,128)} %estimate.1) | data formatting | bytes 524288

commit v3 on v2

--- a/solution.py
+++ b/solution.py
@@ -8,7 +8,11 @@
 from jax.sharding import PartitionSpec as P
 
 ITERS = 2
-UNROLL = (8, 8, 4, 4, 4)
+UNROLL = (8, 8, 4)
+ARRIVALS = (
+    (1, 0), (1, 1), (1, 2), (2, 0), (2, 1), (1, 3), (3, 0),
+    (3, 1), (2, 2), (2, 3), (4, 0), (4, 1), (3, 2), (3, 3),
+)
 LANES = 128
 MESH = pl.DeviceIdType.MESH
 NT = (((1,), (1,)), ((), ()))
@@ -16,16 +20,24 @@
 
 def step_kernel(
     dims,
+    z_hbm,
+    var_hbm,
+    x_hbm,
+    tiles_hbm,
+    pos_hbm,
+    ties_hbm,
+    holder_hbm,
+    hub_hbm,
+    gain_hbm,
+    out_ref,
     z_ref,
     var_ref,
     x_ref,
-    tiles_hbm,
     pos_ref,
     ties_ref,
     holder_ref,
     hub_ref,
-    gain_hbm,
-    out_ref,
+    load_sem,
     tiles,
     gain,
     gain_t,
@@ -52,7 +64,11 @@
     gath,
     us,
     ur,
+    held,
+    part_grad,
     local_sem,
+    x_send,
+    x_recv,
     z_send,
     z_recv,
     v_send,
@@ -87,11 +103,25 @@
     has_upper = a < areas - 1
 
     tiles_copy = pltpu.make_async_copy(
-        tiles_hbm, tiles.at[pl.ds(0, all_tiles)], local_sem.at[0]
+        tiles_hbm, tiles, local_sem.at[0]
     )
     gain_copy = pltpu.make_async_copy(gain_hbm, gain, local_sem.at[1])
-    tiles_copy.start()
-    gain_copy.start()
+    loads = [
+        pltpu.make_async_copy(source, target, load_sem.at[i])
+        for i, (source, target) in enumerate(
+            (
+                (hub_hbm, hub_ref),
+                (z_hbm, z_ref),
+                (var_hbm, var_ref),
+                (x_hbm, x_ref),
+                (ties_hbm, ties_ref),
+                (holder_hbm, holder_ref),
+                (pos_hbm, pos_ref),
+            )
+        )
+    ]
+    for load in loads:
+        load.start()
 
     barrier = pltpu.get_barrier_semaphore()
 
@@ -110,6 +140,11 @@
     lax.fori_loop(1, areas, greet_area, 0)
     lax.fori_loop(1, peers, greet_snap, 0)
 
+    tiles_copy.start()
+    gain_copy.start()
+
+    for load in loads:
+        load.wait()
     lane_a = lax.broadcasted_iota(i32, (areas, LANES), 1)
     for index, listing in enumerate((hub_ref, holder_ref)):
         both = jnp.concatenate([listing[...], listing[...]], axis=1)
@@ -176,6 +211,21 @@
 
     frontier_start(0)
 
+    def rows_copy(i, source):
+        first = pl.multiple_of(lax.rem(s + i, peers) * rows, rows)
+        return pltpu.make_async_remote_copy(
+            src_ref=x_ref.at[:, pl.ds(first, rows)],
+            dst_ref=held.at[0, source],
+            send_sem=x_send.at[i],
+            recv_sem=x_recv.at[source],
+            device_id=(a, lax.rem(s + i, peers)),
+            device_id_type=MESH,
+        )
+
+    for i in range(1, peers):
+        rows_copy(i, s).start()
+    held[0, s] = x_ref[:, pl.ds(pl.multiple_of(s * rows, rows), rows)]
+
     def table_row(index, q):
         even = table[index, pl.ds(2 * q, 1), :]
         odd = table[index, pl.ds(2 * q + 1, 1), :]
@@ -191,7 +241,8 @@
         k = lax.rem(i, tall)
         turn = (k + 1) // 2
         dy = tall // 2 + turn * (1 - 2 * (k % 2))
-        dx = lax.rem(wide // 2 + lax.div(i, tall), wide)
+        group = lax.div(i, tall)
+        dx = lax.rem(wide // 2 + group, wide)
         chip = lax.div(a, 2)
         q = lax.rem(lax.div(chip, wide) + dy, tall) * wide + lax.rem(lax.rem(chip, wide) + dx, wide)
         where_at = table_row(0, q)
@@ -226,7 +277,7 @@
                     src_ref=zs.at[d],
                     dst_ref=zr.at[a],
                     send_sem=z_send,
-                    recv_sem=z_recv,
+                    recv_sem=z_recv.at[group],
                     device_id=(d, s),
                     device_id_type=MESH,
                 ).start()
@@ -234,15 +285,15 @@
                     src_ref=vs.at[q],
                     dst_ref=vr.at[a],
                     send_sem=v_send,
-                    recv_sem=v_recv,
+                    recv_sem=v_recv.at[group],
                     device_id=(d, s),
                     device_id_type=MESH,
                 ).start()
 
             @pl.when(d == a)
             def _():
-                pltpu.make_async_copy(zs.at[d], zr.at[a], z_recv).start()
-                pltpu.make_async_copy(vs.at[q], vr.at[a], v_recv).start()
+                pltpu.make_async_copy(zs.at[d], zr.at[a], z_recv.at[group]).start()
+                pltpu.make_async_copy(vs.at[q], vr.at[a], v_recv.at[group]).start()
 
         return carry
 
@@ -297,44 +348,69 @@
         lax.fori_loop(0, mb, body, 0, unroll=min(mb, UNROLL[1]))
 
     predict(0)
-
-    pltpu.make_async_copy(zr, zr, z_recv).wait()
-    pltpu.make_async_copy(vr, vr, v_recv).wait()
-
-    def unpack(q, carry):
-        even, odd = zr[2 * q], zr[2 * q + 1]
-        arrived[q, pl.ds(0, half)] = jnp.where(lane_h < cap, even, pltpu.roll(odd, cap, 1))
-        arrived[q, pl.ds(half, half)] = jnp.where(lane_h < cap, pltpu.roll(even, cap, 1), odd)
-        return carry
-
-    lax.fori_loop(0, chunks, unpack, 0, unroll=4)
-    variances = jnp.concatenate([vr[c] for c in range(areas)], axis=0)
-    sub_a = lax.broadcasted_iota(i32, (areas, LANES), 0)
+    lax.fori_loop(0, slots, index_tiles, 0)
+    part_grad[all_tiles] = jnp.zeros((snaps, LANES), f32)
+    gain_copy.wait()
+    gain_t[...] = gain[...].T
+
+    my_wide = lax.rem(lax.div(a, 2), wide)
+    batch = zr.at[pl.ds(0, 2 * tall)]
+    batch_v = vr.at[pl.ds(0, 2 * tall)]
+    sub_v = lax.broadcasted_iota(i32, (2 * tall, LANES), 0)
     my_half = lax.rem(a, 2) * cap
-
-    def reorder(j, carry):
-        lane_of = inv_lane[pl.ds(j, 1), :]
-        chunk_of = inv_q[pl.ds(j, 1), :]
-        lanes = jnp.broadcast_to(lane_of, (snaps, LANES))
-        from_chunk = jnp.broadcast_to(chunk_of, (snaps, LANES))
-        taken = jnp.zeros((snaps, LANES), f32)
-        for q in range(chunks):
-            found = jnp.take_along_axis(arrived[q], lanes, axis=1)
-            taken = jnp.where(from_chunk == q, found, taken)
-        z_own[j] = taken
-        hub = 2 * chunk_of + lax.shift_right_arithmetic(lane_of, 6)
-        lane_v = (lane_of & (cap - 1)) + my_half
-        found = jnp.take_along_axis(
-            variances, jnp.broadcast_to(lane_v, (areas, LANES)), axis=1
-        )
-        v_own[pl.ds(j, 1), :] = jnp.sum(
-            jnp.where(jnp.broadcast_to(hub, (areas, LANES)) == sub_a, found, 0.0),
+    for group in range(wide):
+        from_wide = lax.rem(my_wide + 2 * wide - (wide // 2 + group) % wide, wide)
+        pltpu.make_async_copy(batch, batch, z_recv.at[group]).wait()
+        pltpu.make_async_copy(batch_v, batch_v, v_recv.at[group]).wait()
+        variances = jnp.concatenate(
+            [
+                vr[2 * (row * wide + from_wide) + parity]
+                for row in range(tall)
+                for parity in range(2)
+            ],
             axis=0,
-            keepdims=True,
-        )
-        return carry
-
-    lax.fori_loop(0, mb, reorder, 0, unroll=min(mb, UNROLL[3]))
+        )
+
+        def unpack(row, carry):
+            q = row * wide + from_wide
+            even, odd = zr[2 * q], zr[2 * q + 1]
+            arrived[row, pl.ds(0, half)] = jnp.where(
+                lane_h < cap, even, pltpu.roll(odd, cap, 1)
+            )
+            arrived[row, pl.ds(half, half)] = jnp.where(
+                lane_h < cap, pltpu.roll(even, cap, 1), odd
+            )
+            return carry
+
+        lax.fori_loop(0, tall, unpack, 0, unroll=True)
+
+        def reorder(j, carry):
+            lanes = jnp.broadcast_to(inv_lane[pl.ds(j, 1), :], (snaps, LANES))
+            from_chunk = jnp.broadcast_to(inv_q[pl.ds(j, 1), :], (snaps, LANES))
+            taken = jnp.zeros((snaps, LANES), f32) if group == 0 else z_own[j]
+            for row in range(tall):
+                found = jnp.take_along_axis(arrived[row], lanes, axis=1)
+                taken = jnp.where(from_chunk == row * wide + from_wide, found, taken)
+            z_own[j] = taken
+            lane_of = inv_lane[pl.ds(j, 1), :]
+            chunk_of = inv_q[pl.ds(j, 1), :]
+            place = 2 * lax.shift_right_arithmetic(chunk_of, wide.bit_length() - 1)
+            place += lax.shift_right_arithmetic(lane_of, 6)
+            place = jnp.where((chunk_of & (wide - 1)) == from_wide, place, -1)
+            found = jnp.take_along_axis(
+                variances,
+                jnp.broadcast_to((lane_of & (cap - 1)) + my_half, (2 * tall, LANES)),
+                axis=1,
+            )
+            part = jnp.sum(
+                jnp.where(jnp.broadcast_to(place, (2 * tall, LANES)) == sub_v, found, 0.0),
+                axis=0,
+                keepdims=True,
+            )
+            v_own[pl.ds(j, 1), :] = part if group == 0 else v_own[pl.ds(j, 1), :] + part
+            return carry
+
+        lax.fori_loop(0, mb, reorder, 0, unroll=min(mb, 4))
 
     def spread_copy(step, i):
         peer = lax.rem(s + i, peers)
@@ -385,6 +461,14 @@
             return range(pieces)
         return range(pieces // 2) if way == 0 else range(pieces // 2, pieces)
 
+    def piece_of(way, turn):
+        return turn if way == 0 else (turn + pieces // 2) % pieces
+
+    arrivals = [(hop, turn) for hop in range(1, reach) for turn in range(pieces)]
+    arrivals += [(reach, turn) for turn in range(pieces // 2)]
+    if (reach, pieces) == (4, 4):
+        arrivals = ARRIVALS
+
     def came_from(way, hop):
         return lax.rem(s + peers - hop, peers) if way == 0 else lax.rem(s + hop, peers)
 
@@ -398,16 +482,30 @@
             device_id_type=MESH,
         )
 
-    def slot_pair(n2):
-        total = jnp.zeros((snaps, 2 * LANES), f32)
-        for jp in range(mb // 2):
-            left = [tiles[tile_index[2 * n2, 2 * jp + r]] for r in range(2)]
-            right = [tiles[tile_index[2 * n2 + 1, 2 * jp + r]] for r in range(2)]
-            weights = jnp.concatenate(
-                [jnp.concatenate(left, axis=0), jnp.concatenate(right, axis=0)], axis=1
-            )
-            total += jnp.dot(wgt[jp], weights, preferred_element_type=f32)
-        return total
+    def tile_products():
+        def body(j, carry):
+            for k in range(0, touched, 2):
+                pair = jnp.dot(
+                    wgt[j],
+                    jnp.concatenate(
+                        [tiles[j * touched + k], tiles[j * touched + k + 1]], axis=1
+                    ),
+                    preferred_element_type=f32,
+                )
+                part_grad[j * touched + k] = pair[:, :LANES]
+                part_grad[j * touched + k + 1] = pair[:, LANES:]
+            return carry
+
+        lax.fori_loop(0, mb, body, 0, unroll=min(mb, 8))
+
+    def slot_sum(n):
+        terms = [part_grad[tile_index[n, j]] for j in range(mb)]
+        while len(terms) > 1:
+            terms = [
+                terms[i] + terms[i + 1] if i + 1 < len(terms) else terms[i]
+                for i in range(0, len(terms), 2)
+            ]
+        return terms[0]
 
     def gain_piece(step, chunk, piece):
         total = jnp.zeros((snaps, rows), f32)
@@ -419,6 +517,12 @@
             )
         return total
 
+    def returned(step, chunk, update):
+        if step + 1 < ITERS:
+            held[1, chunk] = update
+            return (held[0, chunk] + update).astype(bf16)
+        return (held[1, chunk] + update).astype(bf16)
+
     for step in range(ITERS):
         if step > 0:
             frontier_start(step)
@@ -432,11 +536,6 @@
             )
         for i in range(1, peers):
             spread_copy(step, i).start()
-        if step == 0:
-            lax.fori_loop(0, slots, index_tiles, 0)
-            tiles[all_tiles] = jnp.zeros((LANES, LANES), bf16)
-            gain_copy.wait()
-            gain_t[...] = gain[...].T
         for i in range(1, peers):
             spread_wait(step, i)
         total = ssr[step, 0]
@@ -444,27 +543,23 @@
             total += ssr[step, i]
         scale = v_own[...] + total / snaps_all
         for j in range(mb):
-            wgt[j // 2, :, (j % 2) * LANES : (j % 2 + 1) * LANES] = (
-                resid[j] / scale[j : j + 1, :]
-            ).astype(bf16)
-
+            wgt[j] = (resid[j] / scale[j : j + 1, :]).astype(bf16)
+
+        tile_products()
         for side in range(2):
             for part in range(ties // 2):
-                pair = slot_pair(nb // 2 + side * (ties // 2) + part)
-                bs[step, side, 2 * part] = pair[:, :LANES]
-                bs[step, side, 2 * part + 1] = pair[:, LANES:]
+                for t in (2 * part, 2 * part + 1):
+                    bs[step, side, t] = slot_sum(nb + side * ties + t)
 
                 @pl.when(has_lower if side == 0 else has_upper)
                 def _():
                     boundary_copy(step, side, part).start()
 
-        def own_slots(n2, carry):
-            pair = slot_pair(n2)
-            grads[2 * n2] = pair[:, :LANES]
-            grads[2 * n2 + 1] = pair[:, LANES:]
+        def own_slots(n, carry):
+            grads[n] = slot_sum(n)
             return carry
 
-        lax.fori_loop(0, nb // 2, own_slots, 0, unroll=min(nb // 2, UNROLL[4]))
+        lax.fori_loop(0, nb, own_slots, 0, unroll=4)
 
         @pl.when(has_upper)
         def _():
@@ -476,47 +571,49 @@
             for part in range(ties // 2):
                 boundary_copy(step, 1, part).wait_recv()
 
-        for block in range(nb):
-            total = grads[block]
-            for side in range(2):
-                which = ties
-                for t in range(ties):
-                    which = jnp.where(ties_ref[side, t] == block, t, which)
-                total += br[step, side, which]
-            gath[step, s, block // 2, :, (block % 2) * LANES : (block % 2 + 1) * LANES] = (
-                total.astype(bf16)
-            )
-            if block % (2 * piece_units) == 2 * piece_units - 1:
-                for way in range(2):
-                    ring_copy(step, way, 1, block // (2 * piece_units), s).start()
+        for turn in range(pieces // 2):
+            for way in range(2):
+                piece = piece_of(way, turn)
+                for block in range(2 * piece_units * piece, 2 * piece_units * (piece + 1)):
+                    total = grads[block]
+                    for side in range(2):
+                        which = ties
+                        for t in range(ties):
+                            which = jnp.where(ties_ref[side, t] == block, t, which)
+                        total += br[step, side, which]
+                    first = (block % 2) * LANES
+                    gath[step, s, block // 2, :, first : first + LANES] = total.astype(bf16)
+                ring_copy(step, way, 1, piece, s).start()
+        for turn in range(pieces // 2, pieces):
+            for way in range(2):
+                ring_copy(step, way, 1, piece_of(way, turn), s).start()
 
         own = gain_piece(step, s, 0)
         for piece in range(1, pieces):
             own += gain_piece(step, s, piece)
-        ur[step, s] = own.astype(bf16)
-
-        for hop in range(1, reach + 1):
-            sums = [None, None]
-            for turn in range(len(ring_pieces(0, hop))):
-                for way in range(2):
-                    piece = ring_pieces(way, hop)[turn]
-                    chunk = came_from(way, hop)
-                    ring_copy(step, way, hop, piece, chunk).wait_recv()
-                    if hop < reach and piece in ring_pieces(way, hop + 1):
-                        ring_copy(step, way, hop + 1, piece, chunk).start()
-                for way in range(2):
-                    piece = ring_pieces(way, hop)[turn]
-                    part = gain_piece(step, came_from(way, hop), piece)
-                    sums[way] = part if sums[way] is None else sums[way] + part
-            if hop < reach:
-                for way in range(2):
-                    us[step, came_from(way, hop)] = sums[way].astype(bf16)
-                    update_copy(step, came_from(way, hop)).start()
-            else:
-                us[step, came_from(0, hop)] = (sums[0] + sums[1]).astype(bf16)
-                update_copy(step, came_from(0, hop)).start()
-
-        before = x_ref if step == 0 else out_ref
+        if step == 0:
+            for i in range(1, peers):
+                rows_copy(i, lax.rem(s + i, peers)).wait_recv()
+        ur[step, s] = returned(step, s, own)
+
+        sums = {}
+        for hop, turn in arrivals:
+            for way in range(2):
+                piece = piece_of(way, turn)
+                chunk = came_from(way, hop)
+                ring_copy(step, way, hop, piece, chunk).wait_recv()
+                if hop < reach and piece in ring_pieces(way, hop + 1):
+                    ring_copy(step, way, hop + 1, piece, chunk).start()
+            for way in range(2):
+                chunk = came_from(way, hop)
+                part = gain_piece(step, chunk, piece_of(way, turn))
+                key = (hop, way if hop < reach else 0)
+                count, total = sums.get(key, (0, 0.0))
+                sums[key] = count + 1, total + part
+                if count + 1 == pieces:
+                    us[step, chunk] = returned(step, chunk, total + part)
+                    update_copy(step, chunk).start()
+
         for i in range(peers):
 
             @pl.when(i != s)
@@ -531,15 +628,17 @@
                 ).wait_recv()
 
         for i in range(peers):
-            cols = slice(i * rows, (i + 1) * rows)
-            after = before[:, cols] + ur[step, i].astype(f32)
-            out_ref[:, cols] = after
             if step + 1 < ITERS:
                 for r in range(rows // LANES):
-                    aug[i * (rows // LANES) + r] = after[
-                        :, r * LANES : (r + 1) * LANES
-                    ].astype(bf16)
-
+                    aug[i * (rows // LANES) + r] = ur[
+                        step, i, :, r * LANES : (r + 1) * LANES
+                    ]
+            else:
+                cols = slice(i * rows, (i + 1) * rows)
+                out_ref[:, cols] = x_ref[:, cols] + ur[step, i].astype(f32)
+
+    for i in range(1, peers):
+        rows_copy(i, s).wait_send()
     pltpu.make_async_copy(
         zs.at[pl.ds(0, areas - 1)], zr.at[pl.ds(0, areas - 1)], z_send
     ).wait()
@@ -595,17 +694,24 @@
     pieces = units // 2
     f32, bf16, i32 = jnp.float32, jnp.bfloat16, jnp.int32
     vmem = pl.BlockSpec(memory_space=pltpu.VMEM)
-    smem = pl.BlockSpec(memory_space=pltpu.SMEM)
     hbm = pl.BlockSpec(memory_space=pltpu.HBM)
     dma = pltpu.SemaphoreType.DMA
     dims = (areas, peers, snaps, nb, mb, touched, ties, cap)
     return pl.pallas_call(
         functools.partial(step_kernel, dims),
         out_shape=jax.ShapeDtypeStruct((snaps, states), f32),
-        in_specs=[vmem, vmem, vmem, hbm, smem, smem, vmem, vmem, hbm],
+        in_specs=[hbm] * 9,
         out_specs=vmem,
         scratch_shapes=[
-            pltpu.VMEM((all_tiles + 1, LANES, LANES), bf16),
+            pltpu.VMEM((snaps, mb * LANES), f32),
+            pltpu.VMEM((mb, LANES), f32),
+            pltpu.VMEM((snaps, states), f32),
+            pltpu.SMEM((touched, mb), i32),
+            pltpu.SMEM((2, ties), i32),
+            pltpu.VMEM((areas, cap), i32),
+            pltpu.VMEM((areas, cap), i32),
+            dma((7,)),
+            pltpu.VMEM((all_tiles, LANES, LANES), bf16),
             pltpu.VMEM((rows, states), bf16),
             pltpu.VMEM((states, rows), bf16),
             pltpu.SMEM((slots, mb), i32),
@@ -614,7 +720,7 @@
             pltpu.VMEM((areas, snaps // 2, LANES), f32),
             pltpu.VMEM((chunks, 1, LANES), f32),
             pltpu.VMEM((areas, 1, LANES), f32),
-            pltpu.VMEM((chunks, snaps, LANES), f32),
+            pltpu.VMEM((chunks // min(chunks, 4), snaps, LANES), f32),
             pltpu.VMEM((mb, LANES), i32),
             pltpu.VMEM((mb, LANES), i32),
             pltpu.VMEM((mb, snaps, LANES), f32),
@@ -624,18 +730,22 @@
             pltpu.VMEM((ITERS, 2, ties, snaps, LANES), bf16),
             pltpu.VMEM((mb, snaps, LANES), f32),
             pltpu.VMEM((ITERS, peers, mb, LANES), f32),
-            pltpu.VMEM((mb // 2, snaps, 2 * LANES), bf16),
+            pltpu.VMEM((mb, snaps, LANES), bf16),
             pltpu.VMEM((nb, snaps, LANES), f32),
             pltpu.VMEM((ITERS, 2, ties, snaps, LANES), f32),
             pltpu.VMEM((ITERS, 2, ties + 1, snaps, LANES), f32),
             pltpu.VMEM((ITERS, peers, units, snaps, 2 * LANES), bf16),
             pltpu.VMEM((ITERS, peers, snaps, rows), bf16),
             pltpu.VMEM((ITERS, peers, snaps, rows), bf16),
+            pltpu.VMEM((2, peers, snaps, rows), f32),
+            pltpu.VMEM((all_tiles + 1, snaps, LANES), f32),
             dma((2,)),
+            dma((peers,)),
+            dma((peers,)),
             dma(()),
+            dma((min(chunks, 4),)),
             dma(()),
-            dma(()),
-            dma(()),
+            dma((min(chunks, 4),)),
             dma((ITERS, 2)),
             dma((ITERS, 2)),
             dma((ITERS, peers)),

time: 104 us -> 99.6 us (0.958)
  Pallas kernels: 102 us -> 97.8 us
    pallas_call x1, Pallas kernels: 102 us -> 97.8 us  [on_device(): pl.pallas_call(functools.partial(step_kernel, dims), out_shape=jax.ShapeD...]
where the time goes in v3:
time: 99.6 us; the launch traced here: 99.5 us
  Pallas kernels  97.8 us (98%)
  local copies, waits for them, and re-layouts  1.67 us (2%)
    pallas_call x1, Pallas kernels, on_device(): pl.pallas_call(functools.partial(step_kernel, dims), out_shape=jax.ShapeD...  97.8 us

profile of v3, /device:TPU:8, one launch (start us, length us, event | category | flops | bytes accessed | tf_op | source)
XLA Modules:
  0.0 99.5 jit_solution(7323904470131487942)
XLA Ops:
  0.0 97.8 %estimate.1 = f32[32,2048]{1,0:T(8,128)} custom-call(f32[32,2048]{1,0:T(8,128)} %z_hbm.1, f32[16,128]{1,0:T(8,128)} %bitcast.11, f32[32,2048]{1,0:T(8,128)} %x_hbm.1, bf16[64,128,128]{2,1,0:T(8,128)(2,1)} %bitcast.8, s32[4,16]{1,0:T(4,128)} %bitcast.12, s32[2,4]{1,0:T(2,128)} %bitcast.13, s32[64,64]{1,0:T(8,128)} %bitcast.9, s32[64,64]{1,0:T(8,128)} %bitcast.10, ...), custom_call_target="tpu_custom_call" | custom-call | tf_op jit(solution)/shard_map/estimate/pallas_call | solution.py:700
  97.8 1.7 %copy.11 = f32[32,2048]{1,0:T(8,128)} copy(f32[32,2048]{1,0:T(8,128)} %estimate.1) | data formatting | bytes 524288

commit v4 on v3

--- a/solution.py
+++ b/solution.py
@@ -9,10 +9,8 @@
 
 ITERS = 2
 UNROLL = (8, 8, 4)
-ARRIVALS = (
-    (1, 0), (1, 1), (1, 2), (2, 0), (2, 1), (1, 3), (3, 0),
-    (3, 1), (2, 2), (2, 3), (4, 0), (4, 1), (3, 2), (3, 3),
-)
+GAIN_PARTS = 4
+GAIN_EARLY = 3
 LANES = 128
 MESH = pl.DeviceIdType.MESH
 NT = (((1,), (1,)), ((), ()))
@@ -40,13 +38,10 @@
     load_sem,
     tiles,
     gain,
-    gain_t,
     tile_index,
     table,
     zs,
     zr,
-    vs,
-    vr,
     arrived,
     inv_q,
     inv_lane,
@@ -66,13 +61,13 @@
     ur,
     held,
     part_grad,
+    g_send,
+    g_recv,
     local_sem,
     x_send,
     x_recv,
     z_send,
     z_recv,
-    v_send,
-    v_recv,
     f_send,
     f_recv,
     s_send,
@@ -91,7 +86,6 @@
     units = nb // 2
     piece_units = 2
     pieces = units // piece_units
-    reach = peers // 2
     slots = nb + 2 * ties
     all_tiles = mb * touched
     snaps_all = snaps * peers
@@ -105,7 +99,7 @@
     tiles_copy = pltpu.make_async_copy(
         tiles_hbm, tiles, local_sem.at[0]
     )
-    gain_copy = pltpu.make_async_copy(gain_hbm, gain, local_sem.at[1])
+    gain_copy = pltpu.make_async_copy(gain_hbm, gain.at[0], local_sem.at[1])
     loads = [
         pltpu.make_async_copy(source, target, load_sem.at[i])
         for i, (source, target) in enumerate(
@@ -211,20 +205,53 @@
 
     frontier_start(0)
 
-    def rows_copy(i, source):
-        first = pl.multiple_of(lax.rem(s + i, peers) * rows, rows)
+    ahead = 1 - 2 * lax.rem(a, 2)
+
+    def along(distance):
+        return lax.rem(s + distance * ahead + 2 * peers, peers)
+
+    def block_of_rows(device, index):
+        shift = (0, -1, 1)[index]
+        return lax.rem(device + shift * ahead + peers, peers)
+
+    target = {1: along(3), 2: along(-2)}
+    source = {1: along(-3), 2: along(2)}
+    held_blocks = {0: 3, 1: 3, 2: 2}
+    part_height = rows // GAIN_PARTS
+
+    def gain_copy_to(side, part):
+        where = pl.ds(part * part_height, part_height)
         return pltpu.make_async_remote_copy(
-            src_ref=x_ref.at[:, pl.ds(first, rows)],
-            dst_ref=held.at[0, source],
-            send_sem=x_send.at[i],
-            recv_sem=x_recv.at[source],
-            device_id=(a, lax.rem(s + i, peers)),
+            src_ref=gain_hbm.at[where],
+            dst_ref=gain.at[1 + side, where],
+            send_sem=g_send.at[side, part],
+            recv_sem=g_recv.at[side, part],
+            device_id=(a, along(1) if side == 0 else along(-1)),
             device_id_type=MESH,
         )
 
-    for i in range(1, peers):
-        rows_copy(i, s).start()
-    held[0, s] = x_ref[:, pl.ds(pl.multiple_of(s * rows, rows), rows)]
+    def columns_of(block):
+        return pl.ds(pl.multiple_of(block * rows, rows), rows)
+
+    def rows_copy(role, index):
+        block = block_of_rows(target[role], index)
+        return pltpu.make_async_remote_copy(
+            src_ref=x_ref.at[:, columns_of(block)],
+            dst_ref=held.at[0, role, index],
+            send_sem=x_send.at[role, index],
+            recv_sem=x_recv.at[role, index],
+            device_id=(a, target[role]),
+            device_id_type=MESH,
+        )
+
+    for role in (1, 2):
+        for index in range(held_blocks[role]):
+            rows_copy(role, index).start()
+    for part in range(GAIN_EARLY):
+        for side in range(2):
+            gain_copy_to(side, part).start()
+    for index in range(3):
+        held[0, 0, index] = x_ref[:, columns_of(block_of_rows(s, index))]
 
     def table_row(index, q):
         even = table[index, pl.ds(2 * q, 1), :]
@@ -257,19 +284,20 @@
             )
             taken = jnp.where(from_block == block, found, taken)
         low, high = taken[:half], taken[half:]
-        zs[2 * q] = jnp.where(lane_h < cap, low, pltpu.roll(high, cap, 1))
-        zs[2 * q + 1] = jnp.where(lane_h < cap, pltpu.roll(low, cap, 1), high)
+        zs[2 * q, pl.ds(0, half)] = jnp.where(lane_h < cap, low, pltpu.roll(high, cap, 1))
+        zs[2 * q + 1, pl.ds(0, half)] = jnp.where(lane_h < cap, pltpu.roll(low, cap, 1), high)
         var_found = jnp.take_along_axis(
             var_ref[...], jnp.broadcast_to(lane_of, (mb, LANES)), axis=1
         )
         var_rows = lax.broadcasted_iota(i32, (mb, LANES), 0)
-        vs[q] = jnp.sum(
+        var_row = jnp.sum(
             jnp.where(var_rows == jnp.broadcast_to(block_of, (mb, LANES)), var_found, 0.0),
             axis=0,
             keepdims=True,
         )
         for parity in range(2):
             d = 2 * q + parity
+            zs[d, pl.ds(half, 1)] = var_row
 
             @pl.when(d != a)
             def _():
@@ -281,19 +309,10 @@
                     device_id=(d, s),
                     device_id_type=MESH,
                 ).start()
-                pltpu.make_async_remote_copy(
-                    src_ref=vs.at[q],
-                    dst_ref=vr.at[a],
-                    send_sem=v_send,
-                    recv_sem=v_recv.at[group],
-                    device_id=(d, s),
-                    device_id_type=MESH,
-                ).start()
 
             @pl.when(d == a)
             def _():
                 pltpu.make_async_copy(zs.at[d], zr.at[a], z_recv.at[group]).start()
-                pltpu.make_async_copy(vs.at[q], vr.at[a], v_recv.at[group]).start()
 
         return carry
 
@@ -330,9 +349,7 @@
 
     tiles_copy.wait()
 
-    def predict(step):
-        frontier_wait(step)
-
+    def predict(mine):
         def body(j, carry):
             total = jnp.zeros((snaps, LANES), f32)
             for k in range(touched):
@@ -345,26 +362,24 @@
             resid[j] = total
             return carry
 
-        lax.fori_loop(0, mb, body, 0, unroll=min(mb, UNROLL[1]))
-
-    predict(0)
+        lax.fori_loop(mine.start, mine.stop, body, 0, unroll=min(len(mine), UNROLL[1]))
+
+    frontier_wait(0)
+    predict(range(mb))
     lax.fori_loop(0, slots, index_tiles, 0)
     part_grad[all_tiles] = jnp.zeros((snaps, LANES), f32)
     gain_copy.wait()
-    gain_t[...] = gain[...].T
 
     my_wide = lax.rem(lax.div(a, 2), wide)
     batch = zr.at[pl.ds(0, 2 * tall)]
-    batch_v = vr.at[pl.ds(0, 2 * tall)]
     sub_v = lax.broadcasted_iota(i32, (2 * tall, LANES), 0)
     my_half = lax.rem(a, 2) * cap
     for group in range(wide):
         from_wide = lax.rem(my_wide + 2 * wide - (wide // 2 + group) % wide, wide)
         pltpu.make_async_copy(batch, batch, z_recv.at[group]).wait()
-        pltpu.make_async_copy(batch_v, batch_v, v_recv.at[group]).wait()
         variances = jnp.concatenate(
             [
-                vr[2 * (row * wide + from_wide) + parity]
+                zr[2 * (row * wide + from_wide) + parity, pl.ds(half, 1)]
                 for row in range(tall)
                 for parity in range(2)
             ],
@@ -373,7 +388,7 @@
 
         def unpack(row, carry):
             q = row * wide + from_wide
-            even, odd = zr[2 * q], zr[2 * q + 1]
+            even, odd = zr[2 * q, pl.ds(0, half)], zr[2 * q + 1, pl.ds(0, half)]
             arrived[row, pl.ds(0, half)] = jnp.where(
                 lane_h < cap, even, pltpu.roll(odd, cap, 1)
             )
@@ -412,24 +427,29 @@
 
         lax.fori_loop(0, mb, reorder, 0, unroll=min(mb, 4))
 
-    def spread_copy(step, i):
+    spread_parts = 2 if mb % 16 == 0 else 1
+    part_rows = mb // spread_parts
+
+    def spread_copy(step, i, part):
+        where = pl.ds(part * part_rows, part_rows)
         peer = lax.rem(s + i, peers)
         return pltpu.make_async_remote_copy(
-            src_ref=ssr.at[step, s],
-            dst_ref=ssr.at[step, s],
-            send_sem=s_send.at[step, i],
-            recv_sem=s_recv.at[step, s],
+            src_ref=ssr.at[step, s, where],
+            dst_ref=ssr.at[step, s, where],
+            send_sem=s_send.at[step, i, part],
+            recv_sem=s_recv.at[step, s, part],
             device_id=(a, peer),
             device_id_type=MESH,
         )
 
-    def spread_wait(step, i):
+    def spread_wait(step, i, part):
         source = lax.rem(s + i, peers)
+        where = pl.ds(part * part_rows, part_rows)
         pltpu.make_async_remote_copy(
-            src_ref=ssr.at[step, source],
-            dst_ref=ssr.at[step, source],
-            send_sem=s_send.at[step, i],
-            recv_sem=s_recv.at[step, source],
+            src_ref=ssr.at[step, source, where],
+            dst_ref=ssr.at[step, source, where],
+            send_sem=s_send.at[step, i, part],
+            recv_sem=s_recv.at[step, source, part],
             device_id=(a, source),
             device_id_type=MESH,
         ).wait_recv()
@@ -444,45 +464,28 @@
             device_id_type=MESH,
         )
 
-    def ring_copy(step, way, hop, piece, chunk):
-        beside = lax.rem(s + 1, peers) if way == 0 else lax.rem(s + peers - 1, peers)
+    def chunk_copy(step, role, piece):
         part = pl.ds(piece * piece_units, piece_units)
         return pltpu.make_async_remote_copy(
-            src_ref=gath.at[step, chunk, part],
-            dst_ref=gath.at[step, chunk, part],
-            send_sem=ring_send.at[step, way, hop - 1, piece],
-            recv_sem=ring_recv.at[step, way, hop - 1, piece],
-            device_id=(a, beside),
+            src_ref=gath.at[step, 0, part],
+            dst_ref=gath.at[step, role, part],
+            send_sem=ring_send.at[step, role, piece],
+            recv_sem=ring_recv.at[step, role, piece],
+            device_id=(a, target[role]),
             device_id_type=MESH,
         )
 
-    def ring_pieces(way, hop):
-        if hop < reach:
-            return range(pieces)
-        return range(pieces // 2) if way == 0 else range(pieces // 2, pieces)
-
-    def piece_of(way, turn):
-        return turn if way == 0 else (turn + pieces // 2) % pieces
-
-    arrivals = [(hop, turn) for hop in range(1, reach) for turn in range(pieces)]
-    arrivals += [(reach, turn) for turn in range(pieces // 2)]
-    if (reach, pieces) == (4, 4):
-        arrivals = ARRIVALS
-
-    def came_from(way, hop):
-        return lax.rem(s + peers - hop, peers) if way == 0 else lax.rem(s + hop, peers)
-
-    def update_copy(step, chunk):
+    def update_copy(step, role, index):
         return pltpu.make_async_remote_copy(
-            src_ref=us.at[step, chunk],
-            dst_ref=ur.at[step, s],
-            send_sem=u_send.at[step, chunk],
-            recv_sem=u_recv.at[step, s],
-            device_id=(a, chunk),
+            src_ref=us.at[step, role, index],
+            dst_ref=ur.at[step, block_of_rows(s, index)],
+            send_sem=u_send.at[step, role, index],
+            recv_sem=u_recv.at[step, role, index],
+            device_id=(a, source[role]),
             device_id_type=MESH,
         )
 
-    def tile_products():
+    def tile_products(mine):
         def body(j, carry):
             for k in range(0, touched, 2):
                 pair = jnp.dot(
@@ -496,7 +499,7 @@
                 part_grad[j * touched + k + 1] = pair[:, LANES:]
             return carry
 
-        lax.fori_loop(0, mb, body, 0, unroll=min(mb, 8))
+        lax.fori_loop(mine.start, mine.stop, body, 0, unroll=min(len(mine), 8))
 
     def slot_sum(n):
         terms = [part_grad[tile_index[n, j]] for j in range(mb)]
@@ -507,45 +510,56 @@
             ]
         return terms[0]
 
-    def gain_piece(step, chunk, piece):
-        total = jnp.zeros((snaps, rows), f32)
-        for u in range(piece * piece_units, (piece + 1) * piece_units):
-            total += jnp.dot(
-                gath[step, chunk, u],
-                gain_t[u * 2 * LANES : (u + 1) * 2 * LANES, :],
-                preferred_element_type=f32,
-            )
-        return total
-
-    def returned(step, chunk, update):
+    def gain_piece(step, role, piece, sums):
+        for index in range(held_blocks[role]):
+            for u in range(piece * piece_units, (piece + 1) * piece_units):
+                part = lax.dot_general(
+                    gath[step, role, u],
+                    gain[index, :, u * 2 * LANES : (u + 1) * 2 * LANES],
+                    NT,
+                    preferred_element_type=f32,
+                )
+                sums[role, index] = sums[role, index] + part if (role, index) in sums else part
+
+    def returned(step, role, index, update):
         if step + 1 < ITERS:
-            held[1, chunk] = update
-            return (held[0, chunk] + update).astype(bf16)
-        return (held[1, chunk] + update).astype(bf16)
+            held[1, role, index] = update
+            return (held[0, role, index] + update).astype(bf16)
+        return (held[1, role, index] + update).astype(bf16)
 
     for step in range(ITERS):
         if step > 0:
             frontier_start(step)
-            predict(step)
-
-        for j in range(mb):
-            left_over = z_own[j] - resid[j]
-            resid[j] = left_over
-            ssr[step, s, pl.ds(j, 1), :] = jnp.sum(
-                left_over * left_over, axis=0, keepdims=True
-            )
-        for i in range(1, peers):
-            spread_copy(step, i).start()
-        for i in range(1, peers):
-            spread_wait(step, i)
-        total = ssr[step, 0]
-        for i in range(1, peers):
-            total += ssr[step, i]
-        scale = v_own[...] + total / snaps_all
-        for j in range(mb):
-            wgt[j] = (resid[j] / scale[j : j + 1, :]).astype(bf16)
-
-        tile_products()
+            frontier_wait(step)
+        for part in range(spread_parts):
+            mine = range(part * part_rows, (part + 1) * part_rows)
+            if step > 0:
+                predict(mine)
+            for j in mine:
+                left_over = z_own[j] - resid[j]
+                resid[j] = left_over
+                ssr[step, s, pl.ds(j, 1), :] = jnp.sum(
+                    left_over * left_over, axis=0, keepdims=True
+                )
+            for i in range(1, peers):
+                spread_copy(step, i, part).start()
+        if step == 0:
+            for part in range(GAIN_EARLY, GAIN_PARTS):
+                for side in range(2):
+                    gain_copy_to(side, part).start()
+        for part in range(spread_parts):
+            mine = range(part * part_rows, (part + 1) * part_rows)
+            for i in range(1, peers):
+                spread_wait(step, i, part)
+            where = pl.ds(part * part_rows, part_rows)
+            total = ssr[step, 0, where]
+            for i in range(1, peers):
+                total += ssr[step, i, where]
+            scale = v_own[where, :] + total / snaps_all
+            for j in mine:
+                row = j - part * part_rows
+                wgt[j] = (resid[j] / scale[row : row + 1, :]).astype(bf16)
+            tile_products(mine)
         for side in range(2):
             for part in range(ties // 2):
                 for t in (2 * part, 2 * part + 1):
@@ -571,59 +585,48 @@
             for part in range(ties // 2):
                 boundary_copy(step, 1, part).wait_recv()
 
-        for turn in range(pieces // 2):
-            for way in range(2):
-                piece = piece_of(way, turn)
-                for block in range(2 * piece_units * piece, 2 * piece_units * (piece + 1)):
-                    total = grads[block]
-                    for side in range(2):
-                        which = ties
-                        for t in range(ties):
-                            which = jnp.where(ties_ref[side, t] == block, t, which)
-                        total += br[step, side, which]
-                    first = (block % 2) * LANES
-                    gath[step, s, block // 2, :, first : first + LANES] = total.astype(bf16)
-                ring_copy(step, way, 1, piece, s).start()
-        for turn in range(pieces // 2, pieces):
-            for way in range(2):
-                ring_copy(step, way, 1, piece_of(way, turn), s).start()
-
-        own = gain_piece(step, s, 0)
-        for piece in range(1, pieces):
-            own += gain_piece(step, s, piece)
+        for piece in range(pieces):
+            for block in range(2 * piece_units * piece, 2 * piece_units * (piece + 1)):
+                total = grads[block]
+                for side in range(2):
+                    which = ties
+                    for t in range(ties):
+                        which = jnp.where(ties_ref[side, t] == block, t, which)
+                    total += br[step, side, which]
+                first = (block % 2) * LANES
+                gath[step, 0, block // 2, :, first : first + LANES] = total.astype(bf16)
+            for role in (1, 2):
+                chunk_copy(step, role, piece).start()
+
         if step == 0:
-            for i in range(1, peers):
-                rows_copy(i, lax.rem(s + i, peers)).wait_recv()
-        ur[step, s] = returned(step, s, own)
-
+            for side in range(2):
+                for part in range(GAIN_PARTS):
+                    gain_copy_to(side, part).wait_recv()
+            for role in (1, 2):
+                for index in range(held_blocks[role]):
+                    rows_copy(role, index).wait_recv()
         sums = {}
-        for hop, turn in arrivals:
-            for way in range(2):
-                piece = piece_of(way, turn)
-                chunk = came_from(way, hop)
-                ring_copy(step, way, hop, piece, chunk).wait_recv()
-                if hop < reach and piece in ring_pieces(way, hop + 1):
-                    ring_copy(step, way, hop + 1, piece, chunk).start()
-            for way in range(2):
-                chunk = came_from(way, hop)
-                part = gain_piece(step, chunk, piece_of(way, turn))
-                key = (hop, way if hop < reach else 0)
-                count, total = sums.get(key, (0, 0.0))
-                sums[key] = count + 1, total + part
-                if count + 1 == pieces:
-                    us[step, chunk] = returned(step, chunk, total + part)
-                    update_copy(step, chunk).start()
-
-        for i in range(peers):
-
-            @pl.when(i != s)
-            def _():
+        for piece in range(pieces):
+            gain_piece(step, 0, piece, sums)
+        for index in range(3):
+            ur[step, block_of_rows(s, index)] = returned(step, 0, index, sums[0, index])
+        for piece in range(pieces):
+            for role in (2, 1):
+                chunk_copy(step, role, piece).wait_recv()
+                gain_piece(step, role, piece, sums)
+                if piece + 1 == pieces:
+                    for index in range(held_blocks[role]):
+                        us[step, role, index] = returned(step, role, index, sums[role, index])
+                        update_copy(step, role, index).start()
+        for role in (2, 1):
+            for index in range(held_blocks[role]):
+                block = block_of_rows(target[role], index)
                 pltpu.make_async_remote_copy(
-                    src_ref=us.at[step, i],
-                    dst_ref=ur.at[step, i],
-                    send_sem=u_send.at[step, i],
-                    recv_sem=u_recv.at[step, i],
-                    device_id=(a, i),
+                    src_ref=us.at[step, role, index],
+                    dst_ref=ur.at[step, block],
+                    send_sem=u_send.at[step, role, index],
+                    recv_sem=u_recv.at[step, role, index],
+                    device_id=(a, source[role]),
                     device_id_type=MESH,
                 ).wait_recv()
 
@@ -637,13 +640,14 @@
                 cols = slice(i * rows, (i + 1) * rows)
                 out_ref[:, cols] = x_ref[:, cols] + ur[step, i].astype(f32)
 
-    for i in range(1, peers):
-        rows_copy(i, s).wait_send()
+    for role in (1, 2):
+        for index in range(held_blocks[role]):
+            rows_copy(role, index).wait_send()
+    for side in range(2):
+        for part in range(GAIN_PARTS):
+            gain_copy_to(side, part).wait_send()
     pltpu.make_async_copy(
         zs.at[pl.ds(0, areas - 1)], zr.at[pl.ds(0, areas - 1)], z_send
-    ).wait()
-    pltpu.make_async_copy(
-        vr.at[pl.ds(0, areas - 1)], vr.at[pl.ds(0, areas - 1)], v_send
     ).wait()
     for step in range(ITERS):
 
@@ -660,12 +664,13 @@
                 boundary_copy(step, 1, part).wait_send()
 
         for i in range(1, peers):
-            spread_copy(step, i).wait_send()
-            update_copy(step, lax.rem(s + i, peers)).wait_send()
-        for way in range(2):
-            for hop in range(1, reach + 1):
-                for piece in ring_pieces(way, hop):
-                    ring_copy(step, way, hop, piece, s).wait_send()
+            for part in range(spread_parts):
+                spread_copy(step, i, part).wait_send()
+        for role in (1, 2):
+            for piece in range(pieces):
+                chunk_copy(step, role, piece).wait_send()
+            for index in range(held_blocks[role]):
+                update_copy(step, role, index).wait_send()
 
 
 def on_device(
@@ -690,7 +695,6 @@
     slots = nb + 2 * ties
     all_tiles = mb * touched
     units = nb // 2
-    reach = peers // 2
     pieces = units // 2
     f32, bf16, i32 = jnp.float32, jnp.bfloat16, jnp.int32
     vmem = pl.BlockSpec(memory_space=pltpu.VMEM)
@@ -712,14 +716,11 @@
             pltpu.VMEM((areas, cap), i32),
             dma((7,)),
             pltpu.VMEM((all_tiles, LANES, LANES), bf16),
-            pltpu.VMEM((rows, states), bf16),
-            pltpu.VMEM((states, rows), bf16),
+            pltpu.VMEM((3, rows, states), bf16),
             pltpu.SMEM((slots, mb), i32),
             pltpu.VMEM((2, areas, LANES), i32),
-            pltpu.VMEM((areas, snaps // 2, LANES), f32),
-            pltpu.VMEM((areas, snaps // 2, LANES), f32),
-            pltpu.VMEM((chunks, 1, LANES), f32),
-            pltpu.VMEM((areas, 1, LANES), f32),
+            pltpu.VMEM((areas, snaps // 2 + 1, LANES), f32),
+            pltpu.VMEM((areas, snaps // 2 + 1, LANES), f32),
             pltpu.VMEM((chunks // min(chunks, 4), snaps, LANES), f32),
             pltpu.VMEM((mb, LANES), i32),
             pltpu.VMEM((mb, LANES), i32),
@@ -734,28 +735,28 @@
             pltpu.VMEM((nb, snaps, LANES), f32),
             pltpu.VMEM((ITERS, 2, ties, snaps, LANES), f32),
             pltpu.VMEM((ITERS, 2, ties + 1, snaps, LANES), f32),
-            pltpu.VMEM((ITERS, peers, units, snaps, 2 * LANES), bf16),
+            pltpu.VMEM((ITERS, 3, units, snaps, 2 * LANES), bf16),
+            pltpu.VMEM((ITERS, 3, 3, snaps, rows), bf16),
             pltpu.VMEM((ITERS, peers, snaps, rows), bf16),
-            pltpu.VMEM((ITERS, peers, snaps, rows), bf16),
-            pltpu.VMEM((2, peers, snaps, rows), f32),
+            pltpu.VMEM((2, 3, 3, snaps, rows), f32),
             pltpu.VMEM((all_tiles + 1, snaps, LANES), f32),
+            dma((2, GAIN_PARTS)),
+            dma((2, GAIN_PARTS)),
             dma((2,)),
-            dma((peers,)),
-            dma((peers,)),
-            dma(()),
-            dma((min(chunks, 4),)),
+            dma((3, 3)),
+            dma((3, 3)),
             dma(()),
             dma((min(chunks, 4),)),
             dma((ITERS, 2)),
             dma((ITERS, 2)),
-            dma((ITERS, peers)),
-            dma((ITERS, peers)),
+            dma((ITERS, peers, 2)),
+            dma((ITERS, peers, 2)),
             dma((ITERS, 2, ties // 2)),
             dma((ITERS, 2, ties // 2)),
-            dma((ITERS, 2, reach, pieces)),
-            dma((ITERS, 2, reach, pieces)),
-            dma((ITERS, peers)),
-            dma((ITERS, peers)),
+            dma((ITERS, 3, pieces)),
+            dma((ITERS, 3, pieces)),
+            dma((ITERS, 3, 3)),
+            dma((ITERS, 3, 3)),
         ],
         compiler_params=pltpu.CompilerParams(collective_id=0, has_side_effects=True),
         name="estimate",

time: 99.6 us -> 92.1 us (0.925)
  the two profiles are of different devices: /device:TPU:8 before, /device:TPU:72 now
where the time goes in v4:
time: 92.1 us; the launch traced here: 92 us
  Pallas kernels  90.3 us (98%)
  local copies, waits for them, and re-layouts  1.67 us (2%)
    pallas_call x1, Pallas kernels, on_device(): pl.pallas_call(functools.partial(step_kernel, dims), out_shape=jax.ShapeD...  90.3 us

profile of v4, /device:TPU:72, one launch (start us, length us, event | category | flops | bytes accessed | tf_op | source)
XLA Modules:
  0.0 92.0 jit_solution(12033222565259276815)
XLA Ops:
  0.0 90.3 %estimate.1 = f32[32,2048]{1,0:T(8,128)} custom-call(f32[32,2048]{1,0:T(8,128)} %z_hbm.1, f32[16,128]{1,0:T(8,128)} %bitcast.11, f32[32,2048]{1,0:T(8,128)} %x_hbm.1, bf16[64,128,128]{2,1,0:T(8,128)(2,1)} %bitcast.8, s32[4,16]{1,0:T(4,128)} %bitcast.12, s32[2,4]{1,0:T(2,128)} %bitcast.13, s32[64,64]{1,0:T(8,128)} %bitcast.9, s32[64,64]{1,0:T(8,128)} %bitcast.10, ...), custom_call_target="tpu_custom_call" | custom-call | tf_op jit(solution)/shard_map/estimate/pallas_call | solution.py:704
  90.3 1.7 %copy.11 = f32[32,2048]{1,0:T(8,128)} copy(f32[32,2048]{1,0:T(8,128)} %estimate.1) | data formatting | bytes 524288

commit v5 on v4

--- a/solution.py
+++ b/solution.py
@@ -9,8 +9,8 @@
 
 ITERS = 2
 UNROLL = (8, 8, 4)
-GAIN_PARTS = 4
-GAIN_EARLY = 3
+GAIN_PARTS = 8
+GAIN_EARLY = 5
 LANES = 128
 MESH = pl.DeviceIdType.MESH
 NT = (((1,), (1,)), ((), ()))

time: 92.1 us -> 91.4 us (level)
  the two profiles are of different devices: /device:TPU:72 before, /device:TPU:8 now
where the time goes in v5:
time: 91.4 us; the launch traced here: 91.3 us
  Pallas kernels  89.6 us (98%)
  local copies, waits for them, and re-layouts  1.67 us (2%)
    pallas_call x1, Pallas kernels, on_device(): pl.pallas_call(functools.partial(step_kernel, dims), out_shape=jax.ShapeD...  89.6 us

profile of v5, /device:TPU:8, one launch (start us, length us, event | category | flops | bytes accessed | tf_op | source)
XLA Modules:
  0.0 91.3 jit_solution(12433088580060038922)
XLA Ops:
  0.0 89.6 %estimate.1 = f32[32,2048]{1,0:T(8,128)} custom-call(f32[32,2048]{1,0:T(8,128)} %z_hbm.1, f32[16,128]{1,0:T(8,128)} %bitcast.11, f32[32,2048]{1,0:T(8,128)} %x_hbm.1, bf16[64,128,128]{2,1,0:T(8,128)(2,1)} %bitcast.8, s32[4,16]{1,0:T(4,128)} %bitcast.12, s32[2,4]{1,0:T(2,128)} %bitcast.13, s32[64,64]{1,0:T(8,128)} %bitcast.9, s32[64,64]{1,0:T(8,128)} %bitcast.10, ...), custom_call_target="tpu_custom_call" | custom-call | tf_op jit(solution)/shard_map/estimate/pallas_call | solution.py:704
  89.6 1.7 %copy.11 = f32[32,2048]{1,0:T(8,128)} copy(f32[32,2048]{1,0:T(8,128)} %estimate.1) | data formatting | bytes 524288
